TPU v7x, 256 devices: a whole 4x4x8 slice. The times are simulated.
256 devices in a mesh: tok: 8 (over z), tp: 16 (over y, x), grp: 2 (over core).
Axes of the slice: x: 4, y: 4, z: 8, core: 2. Of those that a mesh axis runs over, the one named last changes fastest.
Arguments:
- hidden: bfloat16 [2048, 6144], P(('tok', 'grp'), 'tp'), may hold values from -6 to 6
- gain: bfloat16 [6144], P('tp'), may hold values from 0.5 to 1.5
- expert_ids: int32 [2048, 2], P(('tok', 'grp')), may hold values from 0 to 7, all different within a row; in each aligned block of 128 rows (0 to 127, 128 to 255, ...) at most 40 rows name the same one
- gate_weights: float32 [2048, 2], P(('tok', 'grp')), may hold values from 0.1 to 0.9
- segment_ids: int32 [2048], P(('tok', 'grp')), may hold values from 0 to 15, never falling along the last dimension, each value on 1 to 384 neighbouring positions
- upstream: bfloat16 [2048, 6144], P(('tok', 'grp'), 'tp'), may hold values from -6 to 6
- w_gate: bfloat16 [8, 6144, 8192], P('tok', None, ('tp', 'grp')), may hold values from -0.078125 to 0.078125
- w_up: bfloat16 [8, 6144, 8192], P('tok', None, ('tp', 'grp')), may hold values from -0.078125 to 0.078125
- w_down: bfloat16 [8, 8192, 6144], P('tok', ('tp', 'grp')), may hold values from -0.0625 to 0.0625
Outputs:
- mixed: bfloat16 [2048, 6144], P(('tok', 'grp'), 'tp')
- importance: float32 [8, 8192], P('tok', ('tp', 'grp'))
Inputs may be any that keep to these rules, and one draw needn't show every extreme that they name: `expert_ids`: each token names 2 different experts. Within the tokens of one token shard (aligned blocks of 128 rows) no expert is named by more than 40 tokens, and in some block one expert is named by exactly 40. `segment_ids`: never falling along the tokens; every document holds between 1 and 384 tokens.
All inputs are finite; a program needn't handle non-finite values.
Results may differ from a plain program's by a relative error of at most 0.0095.
Values may be sent and summed in bfloat16 or wider, within the bound.
No kernel may reach another device: no remote copies, remote signals or barrier semaphores. Data moves between devices by JAX's collectives and lax.ppermute only.
A program may use at most 128 MiB of HBM per device.

v0:
```python
import functools
import math

import jax
import jax.numpy as jnp
from jax import lax
from jax.experimental import pallas as pl
from jax.experimental.pallas import tpu as pltpu
from jax.sharding import PartitionSpec as P


GAIN_ROWS = 16
VMEM_LIMIT = 16 << 20
SCORE_STEPS = ((0, 3), (3, 3), (6, 2))


def plane_shift(value, stage, step):
    side = math.isqrt(lax.axis_size("tp"))
    groups = lax.axis_size("grp")
    pairs = []
    for row in range(side):
        for col in range(side):
            for core in range(groups):
                if (core + stage) % 2 == 0:
                    target = row * side + (col + step) % side
                else:
                    target = ((row + step) % side) * side + col
                pairs.append(((row * side + col) * groups + core, target * groups + core))
    return lax.ppermute(value, ("tp", "grp"), pairs)


def swap_cores(value):
    return lax.ppermute(value, "grp", [(0, 1), (1, 0)])


def plane_gather(own):
    ahead = plane_shift(own, 0, -1)
    behind = plane_shift(own, 0, 1)
    across = plane_shift(own, 0, 2)
    low = jnp.stack([own, ahead])
    high = jnp.stack([across, behind])
    low_behind = plane_shift(low, 1, 1)
    low_ahead = plane_shift(low, 1, -1)
    high_ahead = plane_shift(high, 1, -1)
    high_behind = plane_shift(high, 1, 1)
    low_across = plane_shift(low_behind, 1, 1)
    high_across = plane_shift(high_ahead, 1, -1)
    return [low, high, low_ahead, high_ahead, low_across, high_across, low_behind, high_behind]


def add_wide(*values):
    total = values[0].astype(jnp.float32)
    for value in values[1:]:
        total = total + value.astype(jnp.float32)
    return total.astype(jnp.bfloat16)


def plane_scatter(own, other):
    def piece(at, part):
        span = slice(2 * part, 2 * part + 2)
        return own[at, span], other[at][span]

    low_across = plane_shift(add_wide(*piece(2, 0)), 1, 1)
    high_across = plane_shift(add_wide(*piece(2, 1)), 1, -1)
    to_behind, to_ahead = add_wide(*piece(1, 1)), add_wide(*piece(3, 0))
    high_behind = plane_shift(to_behind, 1, 1)
    low_ahead = plane_shift(to_ahead, 1, -1)
    low_across, _ = lax.optimization_barrier((low_across, to_behind))
    high_across, _ = lax.optimization_barrier((high_across, to_ahead))
    low_behind = plane_shift(add_wide(*piece(1, 0), low_across), 1, 1)
    high_ahead = plane_shift(add_wide(*piece(3, 1), high_across), 1, -1)
    low = (low_behind, low_ahead)
    high = (high_behind, high_ahead)

    def column(at):
        received = low if at < 2 else high
        return add_wide(own[0, at], other[0][at], received[0][at % 2], received[1][at % 2])

    return add_wide(
        column(0),
        plane_shift(column(1), 0, 1),
        plane_shift(column(2), 0, 2),
        plane_shift(column(3), 0, -1),
    )


def columns(x):
    return x[:, :128] + x[:, 128:256] + x[:, 256:384]


def column_specs(units, slice_width, at, which=0):
    return [
        pl.BlockSpec((units, slice_width), lambda s, *t, j=j: (0, t[which][at(s) * 2 + j]))
        for j in range(2)
    ]


def forward_body(rows, width, table, *refs):
    pieces, gate_refs, up_refs, scale_ref = refs[0:8], refs[8:10], refs[10:12], refs[12]
    act_ref, left_ref, slope_ref, lin_ref = refs[13:17]
    gate_acc, up_acc, square_acc, held, sems = refs[17:]
    step = pl.program_id(0)

    def copy(piece, at):
        span = piece.at[:, pl.ds(0, rows + GAIN_ROWS), :]
        return pltpu.make_async_copy(span, held.at[at], sems.at[at])

    @pl.when(step == 0)
    def _():
        for at, piece in enumerate(pieces):
            copy(piece, at).start()
        gate_acc[...] = jnp.zeros_like(gate_acc)
        up_acc[...] = jnp.zeros_like(up_acc)
        square_acc[...] = jnp.zeros_like(square_acc)

    copy(pieces[0], step).wait()
    scaled, squares = [], square_acc[...]
    for j in range(2):
        wide = held[step, j, :rows, :].astype(jnp.float32)
        gain = held[step, j, rows:, :].astype(jnp.float32)[:1, :]
        squares = squares + columns(wide * wide)
        scaled.append((wide * gain).astype(jnp.bfloat16))
    square_acc[...] = squares
    left = jnp.concatenate(scaled, axis=1)
    gate = jnp.concatenate([r[...] for r in gate_refs], axis=0)
    up = jnp.concatenate([r[...] for r in up_refs], axis=0)
    gate_acc[...] += jnp.dot(left, gate, preferred_element_type=jnp.float32)
    up_acc[...] += jnp.dot(left, up, preferred_element_type=jnp.float32)

    @pl.when(step == 7)
    def _():
        total = jnp.sum(square_acc[...], axis=1, keepdims=True)
        scaling = lax.rsqrt(total / width + 1e-05)
        gate_pre = gate_acc[...] * scaling
        up_proj = up_acc[...] * scaling
        sigmoid_gate = jax.nn.sigmoid(gate_pre)
        activated = gate_pre * sigmoid_gate
        act = (activated * up_proj).astype(jnp.bfloat16)
        act_ref[...] = act
        left_ref[...] = (act.astype(jnp.float32) * scale_ref[...]).astype(jnp.bfloat16)
        slope = up_proj * sigmoid_gate * (1.0 + gate_pre * (1.0 - sigmoid_gate))
        scaling = scaling * scale_ref[...]
        slope_ref[...] = slope * scaling
        lin_ref[...] = activated * scaling


def forward(pieces, table, gate_mat, up_mat, row_scale):
    slice_width = pieces[0].shape[2]
    rows = row_scale.shape[0]
    width, units = gate_mat.shape
    row_specs = [
        pl.BlockSpec((slice_width, units), lambda s, t, j=j: (t[s * 2 + j], 0)) for j in range(2)
    ]
    whole = pl.BlockSpec((rows, units), lambda s, t: (0, 0))
    wide = jax.ShapeDtypeStruct((rows, units), jnp.float32)
    narrow = jax.ShapeDtypeStruct((rows, units), jnp.bfloat16)
    return pl.pallas_call(
        functools.partial(forward_body, rows, width),
        out_shape=(narrow, narrow, wide, wide),
        grid_spec=pltpu.PrefetchScalarGridSpec(
            num_scalar_prefetch=1,
            grid=(8,),
            in_specs=[pl.BlockSpec(memory_space=pl.ANY)] * 8
            + row_specs
            + row_specs
            + [pl.BlockSpec((rows, 1), lambda s, t: (0, 0))],
            out_specs=[whole, whole, whole, whole],
            scratch_shapes=[
                pltpu.VMEM((rows, units), jnp.float32),
                pltpu.VMEM((rows, units), jnp.float32),
                pltpu.VMEM((rows, 128), jnp.float32),
                pltpu.VMEM((8, 2, rows + GAIN_ROWS, slice_width), jnp.bfloat16),
                pltpu.SemaphoreType.DMA((8,)),
            ],
        ),
        compiler_params=pltpu.CompilerParams(vmem_limit_bytes=VMEM_LIMIT),
        cost_estimate=pl.CostEstimate(
            flops=4 * rows * width * units, transcendentals=rows * units, bytes_accessed=11 << 20
        ),
        name="forward",
    )(table, *pieces, *([gate_mat] * 2), *([up_mat] * 2), row_scale)


def down_body(table, act_ref, low_ref, high_ref, part_ref):
    for j, ref in enumerate((low_ref, high_ref)):
        part = jnp.dot(act_ref[...], ref[...], preferred_element_type=jnp.float32)
        part_ref[0, j] = part.astype(jnp.bfloat16)


def down(act, table, first, count, down_mat):
    rows, units = act.shape
    slice_width = down_mat.shape[1] // 16

    def at(s):
        return s + 2 * first

    return pl.pallas_call(
        down_body,
        out_shape=jax.ShapeDtypeStruct((count, 4, rows, slice_width), jnp.bfloat16),
        grid_spec=pltpu.PrefetchScalarGridSpec(
            num_scalar_prefetch=1,
            grid=(2 * count,),
            in_specs=[pl.BlockSpec((rows, units), lambda s, t: (0, 0))]
            + column_specs(units, slice_width, at),
            out_specs=pl.BlockSpec((1, 2, rows, slice_width), lambda s, t: (s // 2, s % 2, 0, 0)),
        ),
        compiler_params=pltpu.CompilerParams(vmem_limit_bytes=VMEM_LIMIT),
        cost_estimate=pl.CostEstimate(
            flops=8 * count * rows * units * slice_width,
            transcendentals=0,
            bytes_accessed=count * (2 << 20),
        ),
        name="down",
    )(table, act, down_mat, down_mat)


def grads_body(rows, table, other_table, *refs):
    pieces, own_refs, other_refs = refs[0:16], refs[16:18], refs[18:20]
    act_o, act_p, slope_o, slope_p, lin_o, lin_p = refs[20:26]
    left_ref, acts_ref, grad_acc, held, sems = refs[26:]
    step = pl.program_id(0)

    def copy(piece, at):
        span = piece.at[:, pl.ds(rows + GAIN_ROWS, rows), :]
        return pltpu.make_async_copy(span, held.at[at], sems.at[at])

    @pl.when(step == 0)
    def _():
        for at in range(8):
            copy(pieces[at], at).start()
            copy(pieces[at + 8], at + 8).start()
        grad_acc[...] = jnp.zeros_like(grad_acc)

    dims = (((1,), (1,)), ((), ()))
    copy(pieces[0], step).wait()
    cot = jnp.concatenate([held[step, j] for j in range(2)], axis=1)
    mat = jnp.concatenate([r[...] for r in own_refs], axis=1)
    grad_acc[:rows, :] += lax.dot_general(cot, mat, dims, preferred_element_type=jnp.float32)
    copy(pieces[0], step + 8).wait()
    cot = jnp.concatenate([held[step + 8, j] for j in range(2)], axis=1)
    mat = jnp.concatenate([r[...] for r in other_refs], axis=1)
    grad_acc[rows:, :] += lax.dot_general(cot, mat, dims, preferred_element_type=jnp.float32)

    @pl.when(step == 7)
    def _():
        units = grad_acc.shape[1]
        grad = grad_acc[...]
        slope = jnp.concatenate([slope_o[...], slope_p[...]], axis=0)
        lin = jnp.concatenate([lin_o[...], lin_p[...]], axis=0)
        left_ref[:units, :] = (grad * slope).T.astype(jnp.bfloat16)
        left_ref[units:, :] = (grad * lin).T.astype(jnp.bfloat16)
        act = jnp.concatenate([act_o[...], act_p[...]], axis=0).astype(jnp.float32)
        acts_ref[...] = act.T.astype(jnp.bfloat16)


def activation_grads(tables, pieces, down_mat, saved):
    rows = saved[0].shape[0]
    slice_width = pieces[0].shape[2]
    units, width = down_mat.shape
    whole = pl.BlockSpec((rows, units), lambda s, *t: (0, 0))

    def at(s):
        return s

    return pl.pallas_call(
        functools.partial(grads_body, rows),
        out_shape=(
            jax.ShapeDtypeStruct((2 * units, 2 * rows), jnp.bfloat16),
            jax.ShapeDtypeStruct((units, 2 * rows), jnp.bfloat16),
        ),
        grid_spec=pltpu.PrefetchScalarGridSpec(
            num_scalar_prefetch=2,
            grid=(8,),
            in_specs=[pl.BlockSpec(memory_space=pl.ANY)] * 16
            + column_specs(units, slice_width, at, 0)
            + column_specs(units, slice_width, at, 1)
            + [whole] * 6,
            out_specs=[
                pl.BlockSpec((2 * units, 2 * rows), lambda s, *t: (0, 0)),
                pl.BlockSpec((units, 2 * rows), lambda s, *t: (0, 0)),
            ],
            scratch_shapes=[
                pltpu.VMEM((2 * rows, units), jnp.float32),
                pltpu.VMEM((16, 2, rows, slice_width), jnp.bfloat16),
                pltpu.SemaphoreType.DMA((16,)),
            ],
        ),
        compiler_params=pltpu.CompilerParams(vmem_limit_bytes=VMEM_LIMIT + (4 << 20)),
        cost_estimate=pl.CostEstimate(
            flops=4 * rows * width * units, transcendentals=0, bytes_accessed=14 << 20
        ),
        name="grads",
    )(*tables, *pieces, *([down_mat] * 4), *saved)


def score_body(rows, start, steps, table, left_ref, acts_ref, *refs):
    places = score_pieces(start, steps)
    pieces = dict(zip(places, refs[: len(places)], strict=True))
    refs = refs[len(places) :]
    down_refs, gate_refs, up_refs, out_ref = refs[0:2], refs[2:4], refs[4:6], refs[6]
    own_held, other_held, own_sems, other_sems = refs[7:]
    here = pl.program_id(0)

    @pl.when(here == 0)
    def _():
        for at in range(steps):
            i, h = divmod(start + at, 2)
            pltpu.make_async_copy(
                pieces[0, start + at], own_held.at[at], own_sems.at[at]
            ).start()
            for j in range(2):
                source = pieces[1, 2 * (2 * h + j) + i // 2].at[i % 2]
                pltpu.make_async_copy(source, other_held.at[at, j], other_sems.at[at, j]).start()
        out_ref[...] = jnp.zeros_like(out_ref)

    pltpu.make_async_copy(pieces[0, start], own_held.at[here], own_sems.at[here]).wait()
    units = acts_ref.shape[0]
    cots = rows + GAIN_ROWS
    total = out_ref[...]
    for j in range(2):
        source = pieces[0, start].at[j]
        pltpu.make_async_copy(source, other_held.at[here, j], other_sems.at[here, j]).wait()
        gain = own_held[here, j, rows:cots, :].astype(jnp.float32)[:1, :]
        right = jnp.concatenate([own_held[here, j, :rows, :], other_held[here, j, :rows, :]], axis=0)
        grads = jnp.dot(left_ref[...], right, preferred_element_type=jnp.float32)
        gate = jnp.abs(grads[:units, :] * gate_refs[j][...].astype(jnp.float32))
        up = jnp.abs(grads[units:, :] * up_refs[j][...].astype(jnp.float32))
        total = total + columns((gate + up) * jnp.abs(gain))
        right = jnp.concatenate([own_held[here, j, cots:, :], other_held[here, j, cots:, :]], axis=0)
        grads = jnp.dot(acts_ref[...], right, preferred_element_type=jnp.float32)
        total = total + columns(jnp.abs(grads * down_refs[j][...].astype(jnp.float32)))
    out_ref[...] = total


def score_pieces(start, steps):
    places = [(0, start + at) for at in range(steps)]
    for at in range(steps):
        i, h = divmod(start + at, 2)
        for j in range(2):
            place = (1, 2 * (2 * h + j) + i // 2)
            if place not in places:
                places.append(place)
    return places


def score(start, steps, table, lefts, pieces, mats):
    total_rows, slice_width = pieces[0].shape[1:]
    rows = (total_rows - GAIN_ROWS) // 2
    units = lefts[1].shape[0]
    used = [pieces[8 * side + number] for side, number in score_pieces(start, steps)]

    def at(s):
        return s + start

    down_mat, gate_cols, up_cols = mats
    columns_of = column_specs(units, slice_width, at)
    return pl.pallas_call(
        functools.partial(score_body, rows, start, steps),
        out_shape=jax.ShapeDtypeStruct((units, 128), jnp.float32),
        grid_spec=pltpu.PrefetchScalarGridSpec(
            num_scalar_prefetch=1,
            grid=(steps,),
            in_specs=[
                pl.BlockSpec((2 * units, 2 * rows), lambda s, t: (0, 0)),
                pl.BlockSpec((units, 2 * rows), lambda s, t: (0, 0)),
            ]
            + [pl.BlockSpec(memory_space=pl.ANY)] * len(used)
            + columns_of
            + columns_of
            + columns_of,
            out_specs=pl.BlockSpec((units, 128), lambda s, t: (0, 0)),
            scratch_shapes=[
                pltpu.VMEM((steps, 2, total_rows, slice_width), jnp.bfloat16),
                pltpu.VMEM((steps, 2, total_rows, slice_width), jnp.bfloat16),
                pltpu.SemaphoreType.DMA((steps,)),
                pltpu.SemaphoreType.DMA((steps, 2)),
            ],
        ),
        compiler_params=pltpu.CompilerParams(vmem_limit_bytes=VMEM_LIMIT),
        cost_estimate=pl.CostEstimate(
            flops=12 * rows * units * slice_width * 2 * steps,
            transcendentals=0,
            bytes_accessed=steps * (5 << 19),
        ),
        name="score",
    )(
        table,
        *lefts,
        *used,
        *([down_mat] * 2),
        *([gate_cols] * 2),
        *([up_cols] * 2),
    )


def turn_body(gate_ref, up_ref, gate_out, up_out):
    gate_out[...] = gate_ref[...].T
    up_out[...] = up_ref[...].T


def turned(gate_mat, up_mat):
    width, units = gate_mat.shape
    count = 8
    tall = pl.BlockSpec((width // count, units), lambda s: (s, 0))
    flat = pl.BlockSpec((units, width // count), lambda s: (0, s))
    shape = jax.ShapeDtypeStruct((units, width), gate_mat.dtype)
    return pl.pallas_call(
        turn_body,
        out_shape=(shape, shape),
        grid=(count,),
        in_specs=[tall, tall],
        out_specs=[flat, flat],
        compiler_params=pltpu.CompilerParams(vmem_limit_bytes=VMEM_LIMIT),
        cost_estimate=pl.CostEstimate(flops=0, transcendentals=0, bytes_accessed=12 << 20),
        name="turn",
    )(gate_mat, up_mat)


def on_device(hidden, gain, expert_ids, gate_weights, segment_ids, upstream, w_gate, w_up, w_down):
    rows_here, slice_width = hidden.shape
    top_count = expert_ids.shape[1]
    experts = lax.axis_size("tok")
    groups = lax.axis_size("grp")
    capacity = 5 * rows_here // (2 * experts)
    side = math.isqrt(lax.axis_size("tp"))
    place = lax.axis_index("tp")
    row_at, col_at = place // side, place % side
    outer = jnp.arange(side * side, dtype=jnp.int32) // side
    inner = jnp.arange(side * side, dtype=jnp.int32) % side
    first_core = lax.axis_index("grp") == 0
    row_step = jnp.where(first_core, outer, inner)
    col_step = jnp.where(first_core, inner, outer)
    table = (row_at + row_step) % side * side + (col_at + col_step) % side
    other_table = (row_at + col_step) % side * side + (col_at + row_step) % side

    documents = jnp.arange(experts * groups, dtype=jnp.int32)
    doc_onehot = (segment_ids[:, None] == documents[None, :]).astype(jnp.float32)
    counts = jnp.sum(doc_onehot, axis=0)

    onehot = (
        expert_ids.reshape(-1)[:, None] == jnp.arange(experts, dtype=jnp.int32)[None, :]
    ).astype(jnp.int32)
    before = jnp.cumsum(onehot, axis=0) - onehot
    slot_ids = jnp.sum(before * onehot, axis=1).reshape(rows_here, top_count)

    def matches_of(stride):
        targets = expert_ids * stride + slot_ids
        all_slots = jnp.arange(experts * stride, dtype=jnp.int32)
        return all_slots[:, None, None] == targets[None, :, :]

    def to_experts(block, stride):
        block = block.reshape(experts, stride, slice_width)
        return lax.all_to_all(block, "tok", split_axis=0, concat_axis=0, tiled=True)

    stride = 2 * capacity + 8
    at_slot = jnp.arange(experts * stride, dtype=jnp.int32)
    tokens = jnp.concatenate([hidden, upstream], axis=0)
    targets = expert_ids * stride + slot_ids
    targets = jnp.concatenate([targets, targets + capacity], axis=0)
    placing = jnp.any(at_slot[:, None, None] == targets[None, :, :], axis=2).astype(jnp.bfloat16)
    count_lanes = jnp.pad(counts, (0, slice_width - counts.shape[0]))
    count_rows = jnp.where(
        at_slot[:, None] % stride == 2 * capacity, count_lanes[None, :], 0.0
    )
    blocks = jnp.dot(placing, tokens, preferred_element_type=jnp.float32) + count_rows
    came = to_experts(blocks.astype(jnp.bfloat16), stride)
    came_rows = came[:, :capacity].reshape(experts * capacity, slice_width)
    came_cot = came[:, capacity : 2 * capacity].reshape(experts * capacity, slice_width)
    gain_rows = jnp.broadcast_to(gain[None, :], (GAIN_ROWS, slice_width))
    own_pieces = plane_gather(jnp.concatenate([came_rows, gain_rows, came_cot], axis=0))
    other_pieces = [swap_cores(piece) for piece in own_pieces]

    doc_half = jnp.sum(came[:, 2 * capacity, : counts.shape[0]].astype(jnp.float32), axis=0)
    doc_len = doc_half + swap_cores(doc_half)
    tok_len = jnp.sum(doc_onehot * doc_len[None, :], axis=1)
    tok_weight = rows_here / tok_len
    scaled = gate_weights * tok_weight[:, None]
    matches = matches_of(capacity)
    slot_scale = jnp.sum(jnp.where(matches, scaled[None, :, :], 0.0), axis=(1, 2))
    combining = jnp.sum(jnp.where(matches, gate_weights[None, :, :], 0.0), axis=2)
    scale_own = lax.all_to_all(
        slot_scale.reshape(experts, capacity), "tok", split_axis=0, concat_axis=0, tiled=True
    )
    scale_other = swap_cores(scale_own).reshape(-1, 1)
    scale_own = scale_own.reshape(-1, 1)

    gate_mat, up_mat, down_mat = w_gate[0], w_up[0], w_down[0]
    gate_cols, up_cols = turned(gate_mat, up_mat)
    act_own, left_own, slope_own, lin_own = forward(own_pieces, table, gate_mat, up_mat, scale_own)
    part_own = down(act_own, table, 0, 4, down_mat)
    act_other, left_other, slope_other, lin_other = forward(
        other_pieces, other_table, gate_mat, up_mat, scale_other
    )
    part_other = {}
    for at in (2, 1, 3, 0):
        part = down(act_other, other_table, at, 1, down_mat)
        part_other[at] = swap_cores(part[0])
    outgoing = plane_scatter(part_own, part_other)

    saved = (left_own, left_other, slope_own, slope_other, lin_own, lin_other)
    lefts = activation_grads(
        (table, other_table), own_pieces + other_pieces, down_mat, saved
    )
    scores = 0.0
    for start, steps in SCORE_STEPS:
        scores = scores + score(
            start,
            steps,
            table,
            lefts,
            own_pieces + other_pieces,
            (down_mat, gate_cols, up_cols),
        )
    importance = jnp.sum(scores, axis=1) / (rows_here * experts * groups)

    returned = to_experts(outgoing, capacity)
    returned = returned.reshape(experts * capacity, slice_width).astype(jnp.float32)
    combined = jnp.dot(
        combining.T, returned, precision=lax.Precision.HIGHEST, preferred_element_type=jnp.float32
    )
    mixed = (hidden.astype(jnp.float32) + combined).astype(jnp.bfloat16)
    return (mixed, importance[None, :])


def solution(mesh):
    placed = (
        P(("tok", "grp"), "tp"),
        P("tp"),
        P(("tok", "grp"), None),
        P(("tok", "grp"), None),
        P(("tok", "grp")),
        P(("tok", "grp"), "tp"),
        P("tok", None, ("tp", "grp")),
        P("tok", None, ("tp", "grp")),
        P("tok", ("tp", "grp"), None),
    )
    return jax.shard_map(
        on_device,
        mesh=mesh,
        in_specs=placed,
        out_specs=(P(("tok", "grp"), "tp"), P("tok", ("tp", "grp"))),
        check_vma=False,
    )
```

profile of v0, /device:TPU:1, one launch (start us, length us, event | category | flops | bytes accessed | tf_op | source)
XLA Modules:
  0.0 216.2 jit_solution(10577826218779992477)
XLA Ops:
  4.6 1.3 fusion.1
  5.9 25.2 %all_to_all.22 = bf16[8,88,384]{2,1,0:T(8,128)(2,1)S(1)} all-to-all(bf16[8,88,384]{2,1,0:T(8,128)(2,1)S(1)} %bitcast.174), channel_id=1, replica_groups=mesh['tok'=8,'tp'=16,'grp'=2] {'tok'}, dimensions={0} | all-to-all | bytes 1081344 | tf_op jit(solution)/shard_map/all_to_all | solution.py:453
  31.3 3.0 %collective-permute-start.1 = (bf16[656,384]{1,0:T(8,128)(2,1)S(1)}, bf16[656,384]{1,0:T(8,128)(2,1)S(1)}, u32[]{:S(2)}, u32[]{:S(2)}) collective-permute-start(bf16[656,384]{1,0:T(8,128)(2,1)S(1)} %get-tuple-element.46), channel_id=1, source_target_pairs={{0,4},{1,17},{2,6},{3,19},{4,0},{5,21},{6,2},{7,23},{8,12},{9,25},... | collective-permute-start | bytes 1511432 | tf_op jit(solution)/shard_map/ppermute | solution.py:29
  34.7 2.3 %collective-permute-start = (bf16[656,384]{1,0:T(8,128)(2,1)S(1)}, bf16[656,384]{1,0:T(8,128)(2,1)S(1)}, u32[]{:S(2)}, u32[]{:S(2)}) collective-permute-start(bf16[656,384]{1,0:T(8,128)(2,1)S(1)} %get-tuple-element.46), channel_id=1, source_target_pairs={{0,6},{1,25},{2,0},{3,27},{4,2},{5,29},{6,4},{7,31},{8,14},{9,1},{... | collective-permute-start | bytes 1511432 | tf_op jit(solution)/shard_map/ppermute | solution.py:29
  36.9 4.1 %collective-permute-done.1 = bf16[656,384]{1,0:T(8,128)(2,1)S(1)} collective-permute-done((bf16[656,384]{1,0:T(8,128)(2,1)S(1)}, bf16[656,384]{1,0:T(8,128)(2,1)S(1)}, u32[]{:S(2)}, u32[]{:S(2)}) %collective-permute-start.1) | collective-permute-done | bytes 503840 | tf_op jit(solution)/shard_map/ppermute | solution.py:29
  41.0 5.4 %collective-permute-done.2 = bf16[656,384]{1,0:T(8,128)(2,1)S(1)} collective-permute-done((bf16[656,384]{1,0:T(8,128)(2,1)S(1)}, bf16[656,384]{1,0:T(8,128)(2,1)S(1)}, u32[]{:S(2)}, u32[]{:S(2)}) %collective-permute-start.2) | collective-permute-done | bytes 503840 | tf_op jit(solution)/shard_map/ppermute | solution.py:29
  46.5 2.5 %collective-permute-start.4 = (bf16[2,656,384]{2,1,0:T(8,128)(2,1)S(1)}, bf16[2,656,384]{2,1,0:T(8,128)(2,1)}, u32[]{:S(2)}, u32[]{:S(2)}) collective-permute-start(bf16[2,656,384]{2,1,0:T(8,128)(2,1)S(1)} %pad_maximum_fusion.1.refs_1_), channel_id=1, source_target_pairs={{0,24},{1,7},{2,26},{3,1},{4,28},{5,3},{6,30},{7,5},{8,0},{9,15},{... | collective-permute-start | bytes 3022856 | tf_op jit(solution)/shard_map/ppermute | solution.py:29
  49.4 2.7 %collective-permute-start.3 = (bf16[2,656,384]{2,1,0:T(8,128)(2,1)S(1)}, bf16[2,656,384]{2,1,0:T(8,128)(2,1)}, u32[]{:S(2)}, u32[]{:S(2)}) collective-permute-start(bf16[2,656,384]{2,1,0:T(8,128)(2,1)S(1)} %pad_maximum_fusion.refs_0_), channel_id=1, source_target_pairs={{0,24},{1,7},{2,26},{3,1},{4,28},{5,3},{6,30},{7,5},{8,0},{9,15},{... | collective-permute-start | bytes 3022856 | tf_op jit(solution)/shard_map/ppermute | solution.py:29
  52.0 4.5 %collective-permute-start.9 = (f32[16]{0:T(128)S(1)}, f32[16]{0:T(128)S(1)}, u32[]{:S(2)}, u32[]{:S(2)}) collective-permute-start(f32[16]{0:T(128)S(1)} %fusion.22), channel_id=1, source_target_pairs={{0,1},{1,0},{2,3},{3,2},{4,5},{5,4},{6,7},{7,6},{8,9},{9,8},{10,11... | collective-permute-start | bytes 200 | tf_op jit(solution)/shard_map/ppermute | solution.py:33
  58.3 8.9 %all_to_all.23 = f32[8,1,40]{2,1,0:T(1,128)S(1)} all-to-all(f32[8,1,40]{2,1,0:T(1,128)S(1)} %all_to_all.15), channel_id=1, replica_groups=mesh['tok'=8,'tp'=16,'grp'=2] {'tok'}, dimensions={0} | all-to-all | bytes 2560 | tf_op jit(solution)/shard_map/all_to_all | solution.py:481
  67.2 1.5 collective-permute-start.18
  71.7 3.0 %collective-permute-done.8.refs_7_.refs_1_ = bf16[2,656,384]{2,1,0:T(8,128)(2,1)S(1)} collective-permute-done((bf16[2,656,384]{2,1,0:T(8,128)(2,1)S(1)}, bf16[2,656,384]{2,1,0:T(8,128)(2,1)S(1)}, u32[]{:S(2)}, u32[]{:S(2)}) %collective-permute-start.8) | collective-permute-done | bytes 1007648 | tf_op jit(solution)/shard_map/ppermute | solution.py:29
  74.8 4.8 %collective-permute-start.13 = (bf16[2,656,384]{2,1,0:T(8,128)(2,1)}, bf16[2,656,384]{2,1,0:T(8,128)(2,1)S(1)}, u32[]{:S(2)}, u32[]{:S(2)}) collective-permute-start(bf16[2,656,384]{2,1,0:T(8,128)(2,1)} %collective-permute-done.4.refs_3_.refs_0_), channel_id=1, source_target_pairs={{0,1},{1,0},{2,3},{3,2},{4,5},{5,4},{6,7},{7,6},{8,9},{9,8},{10,11... | collective-permute-start | bytes 3022856 | tf_op jit(solution)/shard_map/ppermute | solution.py:33
  82.5 2.5 %collective-permute-done.7.refs_5_.refs_2_ = bf16[2,656,384]{2,1,0:T(8,128)(2,1)} collective-permute-done((bf16[2,656,384]{2,1,0:T(8,128)(2,1)}, bf16[2,656,384]{2,1,0:T(8,128)(2,1)}, u32[]{:S(2)}, u32[]{:S(2)}) %collective-permute-start.7) | collective-permute-done | bytes 1007648 | tf_op jit(solution)/shard_map/ppermute | solution.py:29
  85.0 1.5 collective-permute-start.12
  86.5 3.3 %collective-permute-done.6.refs_4_.refs_1_ = bf16[2,656,384]{2,1,0:T(8,128)(2,1)} collective-permute-done((bf16[2,656,384]{2,1,0:T(8,128)(2,1)}, bf16[2,656,384]{2,1,0:T(8,128)(2,1)}, u32[]{:S(2)}, u32[]{:S(2)}) %collective-permute-start.6) | collective-permute-done | bytes 1007648 | tf_op jit(solution)/shard_map/ppermute | solution.py:29
  89.8 5.6 %collective-permute-start.15 = (bf16[2,656,384]{2,1,0:T(8,128)(2,1)}, bf16[2,656,384]{2,1,0:T(8,128)(2,1)S(1)}, u32[]{:S(2)}, u32[]{:S(2)}) collective-permute-start(bf16[2,656,384]{2,1,0:T(8,128)(2,1)} %collective-permute-done.7.refs_5_.refs_2_), channel_id=1, source_target_pairs={{0,1},{1,0},{2,3},{3,2},{4,5},{5,4},{6,7},{7,6},{8,9},{9,8},{10,11... | collective-permute-start | bytes 3022856 | tf_op jit(solution)/shard_map/ppermute | solution.py:33
  99.4 1.9 copy-done.5
  101.3 1.9 copy-done.8
  103.2 1.2 copy-done.12
  104.4 1.2 copy-done.16
  105.6 1.2 copy-done.20
  106.9 1.2 copy-done.24
  110.5 5.8 %forward.3 = (bf16[320,256]{1,0:T(8,128)(2,1)S(1)}, bf16[320,256]{1,0:T(8,128)(2,1)S(1)}, f32[320,256]{1,0:T(8,128)S(1)}, f32[320,256]{1,0:T(8,128)S(1)}) custom-call(s32[16]{0:T(128)S(1)} %fusion.27.table.other_table, bf16[2,656,384]{2,1,0:T(8,128)(2,1)S(1)} %copy-done.41, bf16[2,656,384]{2,1,0:T(8,128)(2,1)S(1)} %copy-done.12, ...), custom_call_target="tpu_custom_call" | custom-call | flops 2013265920 | bytes 11534336 | tf_op jit(solution)/shard_map/forward/pallas_call | solution.py:157
  116.3 2.2 %down.7 = bf16[1,4,320,384]{3,2,1,0:T(8,128)(2,1)} custom-call(s32[16]{0:T(128)S(1)} %fusion.27.table.other_table, bf16[320,256]{1,0:T(8,128)(2,1)S(1)} %get-tuple-element.17.act_ref, bf16[256,6144]{1,0:T(8,128)(2,1)S(1)} %bitcast.140, bf16[256,6144]{1,0:T(8,128)(2,1)S(1)} %bitcast.141), custom_call_target="tpu_custom_call" | custom-call | flops 251658240 | bytes 2097152 | tf_op jit(solution)/shard_map/down/pallas_call | solution.py:197
  118.6 2.2 %down.9 = bf16[1,4,320,384]{3,2,1,0:T(8,128)(2,1)} custom-call(s32[16]{0:T(128)S(1)} %fusion.27.table.other_table, bf16[320,256]{1,0:T(8,128)(2,1)S(1)} %get-tuple-element.17.act_ref, bf16[256,6144]{1,0:T(8,128)(2,1)S(1)} %bitcast.142, bf16[256,6144]{1,0:T(8,128)(2,1)S(1)} %bitcast.143), custom_call_target="tpu_custom_call" | custom-call | flops 251658240 | bytes 2097152 | tf_op jit(solution)/shard_map/down/pallas_call | solution.py:197
  120.8 2.2 %down.8 = bf16[1,4,320,384]{3,2,1,0:T(8,128)(2,1)} custom-call(s32[16]{0:T(128)S(1)} %fusion.27.table.other_table, bf16[320,256]{1,0:T(8,128)(2,1)S(1)} %get-tuple-element.17.act_ref, bf16[256,6144]{1,0:T(8,128)(2,1)S(1)} %bitcast.144, bf16[256,6144]{1,0:T(8,128)(2,1)S(1)} %bitcast.145), custom_call_target="tpu_custom_call" | custom-call | flops 251658240 | bytes 2097152 | tf_op jit(solution)/shard_map/down/pallas_call | solution.py:197
  125.3 1.9 copy-done.6
  127.1 1.9 copy-done.9
  132.7 5.2 %forward.2 = (bf16[320,256]{1,0:T(8,128)(2,1)S(1)}, bf16[320,256]{1,0:T(8,128)(2,1)S(1)}, f32[320,256]{1,0:T(8,128)S(1)}, f32[320,256]{1,0:T(8,128)S(1)}) custom-call(s32[16]{0:T(128)S(1)} %fusion.26.table, bf16[2,656,384]{2,1,0:T(8,128)(2,1)S(1)} %copy-done.31, bf16[2,656,384]{2,1,0:T(8,128)(2,1)S(1)} %copy-done.28, ...), custom_call_target="tpu_custom_call" | custom-call | flops 2013265920 | bytes 11534336 | tf_op jit(solution)/shard_map/forward/pallas_call | solution.py:157
  137.9 3.8 %down.5 = bf16[4,4,320,384]{3,2,1,0:T(8,128)(2,1)S(1)} custom-call(s32[16]{0:T(128)S(1)} %fusion.26.table, bf16[320,256]{1,0:T(8,128)(2,1)S(1)} %get-tuple-element.16.act_ref, bf16[256,6144]{1,0:T(8,128)(2,1)S(1)} %bitcast.146, bf16[256,6144]{1,0:T(8,128)(2,1)S(1)} %bitcast.147), custom_call_target="tpu_custom_call" | custom-call | flops 1006632960 | bytes 8388608 | tf_op jit(solution)/shard_map/down/pallas_call | solution.py:197
  141.7 2.0 fusion.8
  144.1 1.4 collective-permute-start.22
  145.6 1.4 down.6
  149.0 3.0 %collective-permute-done.28 = bf16[2,320,384]{2,1,0:T(8,128)(2,1)S(1)} collective-permute-done((bf16[2,320,384]{2,1,0:T(8,128)(2,1)S(1)}, bf16[2,320,384]{2,1,0:T(8,128)(2,1)S(1)}, u32[]{:S(2)}, u32[]{:S(2)}) %collective-permute-start.28) | collective-permute-done | bytes 491552 | tf_op jit(solution)/shard_map/ppermute | solution.py:29
  152.0 1.3 collective-permute-done.22
  153.3 1.7 fusion.10
  155.3 2.5 %collective-permute-start.29 = (bf16[2,320,384]{2,1,0:T(8,128)(2,1)S(1)}, bf16[2,320,384]{2,1,0:T(8,128)(2,1)S(1)}, u32[]{:S(2)}, u32[]{:S(2)}) collective-permute-start(bf16[2,320,384]{2,1,0:T(8,128)(2,1)S(1)} %get-tuple-element.40), channel_id=1, source_target_pairs={{0,24},{1,7},{2,26},{3,1},{4,28},{5,3},{6,30},{7,5},{8,0},{9,15},{... | collective-permute-start | bytes 1474568 | tf_op jit(solution)/shard_map/ppermute | solution.py:29
  157.8 2.5 %turn.1 = (bf16[256,6144]{1,0:T(8,128)(2,1)S(1)}, bf16[256,6144]{1,0:T(8,128)(2,1)S(1)}) custom-call(bf16[6144,256]{1,0:T(8,128)(2,1)S(1)} %bitcast.164, bf16[6144,256]{1,0:T(8,128)(2,1)S(1)} %bitcast.169), custom_call_target="tpu_custom_call" | custom-call | bytes 12582912 | tf_op jit(solution)/shard_map/turn/pallas_call | solution.py:407
  160.5 10.9 %grads.1 = (bf16[512,640]{1,0:T(8,128)(2,1)S(1)}, bf16[256,640]{1,0:T(8,128)(2,1)S(1)}) custom-call(s32[16]{0:T(128)S(1)} %fusion.26.table, s32[16]{0:T(128)S(1)} %fusion.27.table.other_table, bf16[2,656,384]{2,1,0:T(8,128)(2,1)S(1)} %copy-done.32, bf16[2,656,384]{2,1,0:T(8,128)(2,1)S(1)} %copy-done.29, bf16[2,656,384]{2,1,0:T(8,128)(2,1)} %collective-permute-done.3.refs_2_, ...), custom_call_target="tpu_custom_call" | custom-call | flops 2013265920 | bytes 14680064 | tf_op jit(solution)/shard_map/grads/pallas_call | solution.py:265
  172.0 1.6 collective-permute-start.30
  174.6 7.9 %score.4 = f32[256,128]{1,0:T(8,128)S(1)} custom-call(s32[16]{0:T(128)S(1)} %fusion.26.table, bf16[512,640]{1,0:T(8,128)(2,1)S(1)} %get-tuple-element.26.left_ref, bf16[256,640]{1,0:T(8,128)(2,1)S(1)} %get-tuple-element.27.acts_ref, bf16[2,656,384]{2,1,0:T(8,128)(2,1)} %collective-permute-done.4.refs_3_.refs_0_, ...), custom_call_target="tpu_custom_call" | custom-call | flops 2264924160 | bytes 7864320 | tf_op jit(solution)/shard_map/score/pallas_call | solution.py:357
  183.3 8.0 %score.3 = f32[256,128]{1,0:T(8,128)S(1)} custom-call(s32[16]{0:T(128)S(1)} %fusion.26.table, bf16[512,640]{1,0:T(8,128)(2,1)S(1)} %get-tuple-element.26.left_ref, bf16[256,640]{1,0:T(8,128)(2,1)S(1)} %get-tuple-element.27.acts_ref, bf16[2,656,384]{2,1,0:T(8,128)(2,1)S(1)} %copy-done.32, bf16[2,656,384]{2,1,0:T(8,128)(2,1)S(1)} %copy-done.29, ...), custom_call_target="tpu_custom_call" | custom-call | flops 2264924160 | bytes 7864320 | tf_op jit(solution)/shard_map/score/pallas_call | solution.py:357
  192.2 4.0 %all-to-all-start.2 = ((bf16[8,40,384]{2,1,0:T(8,128)(2,1)}), bf16[8,40,384]{2,1,0:T(8,128)(2,1)}, u32[]{:S(2)}, u32[]{:S(2)}) async-start(bf16[8,40,384]{2,1,0:T(8,128)(2,1)} %bitcast.171), calls=%async_computation.2 | async-start | bytes 491520 | tf_op jit(solution)/shard_map/all_to_all | solution.py:453
  196.3 1.9 copy-done.2
  198.2 1.9 copy-done.4
  207.2 6.2 %score.5 = f32[256,128]{1,0:T(8,128)S(1)} custom-call(s32[16]{0:T(128)S(1)} %fusion.26.table, bf16[512,640]{1,0:T(8,128)(2,1)S(1)} %copy-done.44, bf16[256,640]{1,0:T(8,128)(2,1)S(1)} %get-tuple-element.27.acts_ref, bf16[2,656,384]{2,1,0:T(8,128)(2,1)} %collective-permute-done.5.refs_6_.refs_0_, bf16[2,656,384]{2,1,0:T(8,128)(2,1)S(1)} %copy-done.39, ...), custom_call_target="tpu_custom_call" | custom-call | flops 1509949440 | bytes 5242880 | tf_op jit(solution)/shard_map/score/pallas_call | solution.py:357
  214.1 2.2 fusion.2
  (191 shorter events, 38.9 us)
Async XLA Ops:
  0.6 30.5 %copy-start.56 = (bf16[384]{0:T(512)(128)(2,1)S(1)}, bf16[384]{0:T(512)(128)(2,1)}, u32[]{:S(2)}) copy-start(bf16[384]{0:T(512)(128)(2,1)} %param.10) | copy-start | bytes 2308
  31.1 26.3 %copy-start.57 = (s32[128]{0:T(128)S(1)}, s32[128]{0:T(128)}, u32[]{:S(2)}) copy-start(s32[128]{0:T(128)} %param.13) | copy-start | bytes 1540
  31.1 26.3 %copy-start.55 = (f32[128,2]{0,1:T(2,128)S(1)}, f32[128,2]{0,1:T(2,128)}, u32[]{:S(2)}) copy-start(f32[128,2]{0,1:T(2,128)} %param.12) | copy-start | bytes 3076
  31.3 9.7 %collective-permute-start.1 = (bf16[656,384]{1,0:T(8,128)(2,1)S(1)}, bf16[656,384]{1,0:T(8,128)(2,1)S(1)}, u32[]{:S(2)}, u32[]{:S(2)}) collective-permute-start(bf16[656,384]{1,0:T(8,128)(2,1)S(1)} %get-tuple-element.46), channel_id=1, source_target_pairs={{0,4},{1,17},{2,6},{3,19},{4,0},{5,21},{6,2},{7,23},{8,12},{9,25},... | collective-permute-start | bytes 1511432 | tf_op jit(solution)/shard_map/ppermute | solution.py:29
  34.3 12.1 %collective-permute-start.2 = (bf16[656,384]{1,0:T(8,128)(2,1)S(1)}, bf16[656,384]{1,0:T(8,128)(2,1)S(1)}, u32[]{:S(2)}, u32[]{:S(2)}) collective-permute-start(bf16[656,384]{1,0:T(8,128)(2,1)S(1)} %get-tuple-element.46), channel_id=1, source_target_pairs={{0,2},{1,9},{2,4},{3,11},{4,6},{5,13},{6,0},{7,15},{8,10},{9,17},{... | collective-permute-start | bytes 1511432 | tf_op jit(solution)/shard_map/ppermute | solution.py:29
  34.7 14.4 %collective-permute-start = (bf16[656,384]{1,0:T(8,128)(2,1)S(1)}, bf16[656,384]{1,0:T(8,128)(2,1)S(1)}, u32[]{:S(2)}, u32[]{:S(2)}) collective-permute-start(bf16[656,384]{1,0:T(8,128)(2,1)S(1)} %get-tuple-element.46), channel_id=1, source_target_pairs={{0,6},{1,25},{2,0},{3,27},{4,2},{5,29},{6,4},{7,31},{8,14},{9,1},{... | collective-permute-start | bytes 1511432 | tf_op jit(solution)/shard_map/ppermute | solution.py:29
  46.5 35.0 %copy-start.27 = (bf16[2,656,384]{2,1,0:T(8,128)(2,1)}, bf16[2,656,384]{2,1,0:T(8,128)(2,1)S(1)}, u32[]{:S(2)}) copy-start(bf16[2,656,384]{2,1,0:T(8,128)(2,1)S(1)} %pad_maximum_fusion.1.refs_1_) | copy-start | bytes 3022852
  46.5 23.3 %collective-permute-start.4 = (bf16[2,656,384]{2,1,0:T(8,128)(2,1)S(1)}, bf16[2,656,384]{2,1,0:T(8,128)(2,1)}, u32[]{:S(2)}, u32[]{:S(2)}) collective-permute-start(bf16[2,656,384]{2,1,0:T(8,128)(2,1)S(1)} %pad_maximum_fusion.1.refs_1_), channel_id=1, source_target_pairs={{0,24},{1,7},{2,26},{3,1},{4,28},{5,3},{6,30},{7,5},{8,0},{9,15},{... | collective-permute-start | bytes 3022856 | tf_op jit(solution)/shard_map/ppermute | solution.py:29
  49.2 21.8 %collective-permute-start.5 = (bf16[2,656,384]{2,1,0:T(8,128)(2,1)S(1)}, bf16[2,656,384]{2,1,0:T(8,128)(2,1)}, u32[]{:S(2)}, u32[]{:S(2)}) collective-permute-start(bf16[2,656,384]{2,1,0:T(8,128)(2,1)S(1)} %pad_maximum_fusion.refs_0_), channel_id=1, source_target_pairs={{0,8},{1,3},{2,10},{3,5},{4,12},{5,7},{6,14},{7,1},{8,16},{9,11},{... | collective-permute-start | bytes 3022856 | tf_op jit(solution)/shard_map/ppermute | solution.py:29
  49.3 25.5 %collective-permute-start.8 = (bf16[2,656,384]{2,1,0:T(8,128)(2,1)S(1)}, bf16[2,656,384]{2,1,0:T(8,128)(2,1)S(1)}, u32[]{:S(2)}, u32[]{:S(2)}) collective-permute-start(bf16[2,656,384]{2,1,0:T(8,128)(2,1)S(1)} %pad_maximum_fusion.1.refs_1_), channel_id=1, source_target_pairs={{0,8},{1,3},{2,10},{3,5},{4,12},{5,7},{6,14},{7,1},{8,16},{9,11},{... | collective-permute-start | bytes 3022856 | tf_op jit(solution)/shard_map/ppermute | solution.py:29
  49.4 25.4 %collective-permute-start.3 = (bf16[2,656,384]{2,1,0:T(8,128)(2,1)S(1)}, bf16[2,656,384]{2,1,0:T(8,128)(2,1)}, u32[]{:S(2)}, u32[]{:S(2)}) collective-permute-start(bf16[2,656,384]{2,1,0:T(8,128)(2,1)S(1)} %pad_maximum_fusion.refs_0_), channel_id=1, source_target_pairs={{0,24},{1,7},{2,26},{3,1},{4,28},{5,3},{6,30},{7,5},{8,0},{9,15},{... | collective-permute-start | bytes 3022856 | tf_op jit(solution)/shard_map/ppermute | solution.py:29
  52.0 5.3 %collective-permute-start.9 = (f32[16]{0:T(128)S(1)}, f32[16]{0:T(128)S(1)}, u32[]{:S(2)}, u32[]{:S(2)}) collective-permute-start(f32[16]{0:T(128)S(1)} %fusion.22), channel_id=1, source_target_pairs={{0,1},{1,0},{2,3},{3,2},{4,5},{5,4},{6,7},{7,6},{8,9},{9,8},{10,11... | collective-permute-start | bytes 200 | tf_op jit(solution)/shard_map/ppermute | solution.py:33
  67.2 2.3 %collective-permute-start.18 = (f32[8,40]{1,0:T(8,128)S(1)}, f32[8,40]{1,0:T(8,128)S(1)}, u32[]{:S(2)}, u32[]{:S(2)}) collective-permute-start(f32[8,40]{1,0:T(8,128)S(1)} %bitcast.178), channel_id=1, source_target_pairs={{0,1},{1,0},{2,3},{3,2},{4,5},{5,4},{6,7},{7,6},{8,9},{9,8},{10,11... | collective-permute-start | bytes 3848 | tf_op jit(solution)/shard_map/ppermute | solution.py:33
  69.5 10.1 %collective-permute-start.11 = (bf16[2,656,384]{2,1,0:T(8,128)(2,1)S(1)}, bf16[2,656,384]{2,1,0:T(8,128)(2,1)S(1)}, u32[]{:S(2)}, u32[]{:S(2)}) collective-permute-start(bf16[2,656,384]{2,1,0:T(8,128)(2,1)S(1)} %pad_maximum_fusion.1.refs_1_), channel_id=1, source_target_pairs={{0,1},{1,0},{2,3},{3,2},{4,5},{5,4},{6,7},{7,6},{8,9},{9,8},{10,11... | collective-permute-start | bytes 3022856 | tf_op jit(solution)/shard_map/ppermute | solution.py:33
  69.9 11.6 %collective-permute-start.10 = (bf16[2,656,384]{2,1,0:T(8,128)(2,1)S(1)}, bf16[2,656,384]{2,1,0:T(8,128)(2,1)S(1)}, u32[]{:S(2)}, u32[]{:S(2)}) collective-permute-start(bf16[2,656,384]{2,1,0:T(8,128)(2,1)S(1)} %pad_maximum_fusion.refs_0_), channel_id=1, source_target_pairs={{0,1},{1,0},{2,3},{3,2},{4,5},{5,4},{6,7},{7,6},{8,9},{9,8},{10,11... | collective-permute-start | bytes 3022856 | tf_op jit(solution)/shard_map/ppermute | solution.py:33
  71.0 14.0 %collective-permute-start.7 = (bf16[2,656,384]{2,1,0:T(8,128)(2,1)}, bf16[2,656,384]{2,1,0:T(8,128)(2,1)}, u32[]{:S(2)}, u32[]{:S(2)}) collective-permute-start(bf16[2,656,384]{2,1,0:T(8,128)(2,1)} %collective-permute-done.4.refs_3_.refs_0_), channel_id=1, source_target_pairs={{0,24},{1,7},{2,26},{3,1},{4,28},{5,3},{6,30},{7,5},{8,0},{9,15},{... | collective-permute-start | bytes 3022856 | tf_op jit(solution)/shard_map/ppermute | solution.py:29
  74.8 15.0 %collective-permute-start.6 = (bf16[2,656,384]{2,1,0:T(8,128)(2,1)}, bf16[2,656,384]{2,1,0:T(8,128)(2,1)}, u32[]{:S(2)}, u32[]{:S(2)}) collective-permute-start(bf16[2,656,384]{2,1,0:T(8,128)(2,1)} %collective-permute-done.5.refs_6_.refs_0_), channel_id=1, source_target_pairs={{0,8},{1,3},{2,10},{3,5},{4,12},{5,7},{6,14},{7,1},{8,16},{9,11},{... | collective-permute-start | bytes 3022856 | tf_op jit(solution)/shard_map/ppermute | solution.py:29
  74.8 20.6 %collective-permute-start.13 = (bf16[2,656,384]{2,1,0:T(8,128)(2,1)}, bf16[2,656,384]{2,1,0:T(8,128)(2,1)S(1)}, u32[]{:S(2)}, u32[]{:S(2)}) collective-permute-start(bf16[2,656,384]{2,1,0:T(8,128)(2,1)} %collective-permute-done.4.refs_3_.refs_0_), channel_id=1, source_target_pairs={{0,1},{1,0},{2,3},{3,2},{4,5},{5,4},{6,7},{7,6},{8,9},{9,8},{10,11... | collective-permute-start | bytes 3022856 | tf_op jit(solution)/shard_map/ppermute | solution.py:33
  80.5 17.0 %collective-permute-start.16 = (bf16[2,656,384]{2,1,0:T(8,128)(2,1)}, bf16[2,656,384]{2,1,0:T(8,128)(2,1)S(1)}, u32[]{:S(2)}, u32[]{:S(2)}) collective-permute-start(bf16[2,656,384]{2,1,0:T(8,128)(2,1)} %collective-permute-done.5.refs_6_.refs_0_), channel_id=1, source_target_pairs={{0,1},{1,0},{2,3},{3,2},{4,5},{5,4},{6,7},{7,6},{8,9},{9,8},{10,11... | collective-permute-start | bytes 3022856 | tf_op jit(solution)/shard_map/ppermute | solution.py:33
  82.5 13.9 %collective-permute-start.17 = (bf16[2,656,384]{2,1,0:T(8,128)(2,1)}, bf16[2,656,384]{2,1,0:T(8,128)(2,1)S(1)}, u32[]{:S(2)}, u32[]{:S(2)}) collective-permute-start(bf16[2,656,384]{2,1,0:T(8,128)(2,1)} %copy-done.36), channel_id=1, source_target_pairs={{0,1},{1,0},{2,3},{3,2},{4,5},{5,4},{6,7},{7,6},{8,9},{9,8},{10,11... | collective-permute-start | bytes 3022856 | tf_op jit(solution)/shard_map/ppermute | solution.py:33
  85.0 13.5 %collective-permute-start.12 = (bf16[2,656,384]{2,1,0:T(8,128)(2,1)}, bf16[2,656,384]{2,1,0:T(8,128)(2,1)}, u32[]{:S(2)}, u32[]{:S(2)}) collective-permute-start(bf16[2,656,384]{2,1,0:T(8,128)(2,1)} %collective-permute-done.3.refs_2_), channel_id=1, source_target_pairs={{0,1},{1,0},{2,3},{3,2},{4,5},{5,4},{6,7},{7,6},{8,9},{9,8},{10,11... | collective-permute-start | bytes 3022856 | tf_op jit(solution)/shard_map/ppermute | solution.py:33
  89.8 8.7 %collective-permute-start.15 = (bf16[2,656,384]{2,1,0:T(8,128)(2,1)}, bf16[2,656,384]{2,1,0:T(8,128)(2,1)S(1)}, u32[]{:S(2)}, u32[]{:S(2)}) collective-permute-start(bf16[2,656,384]{2,1,0:T(8,128)(2,1)} %collective-permute-done.7.refs_5_.refs_2_), channel_id=1, source_target_pairs={{0,1},{1,0},{2,3},{3,2},{4,5},{5,4},{6,7},{7,6},{8,9},{9,8},{10,11... | collective-permute-start | bytes 3022856 | tf_op jit(solution)/shard_map/ppermute | solution.py:33
  96.3 3.1 %collective-permute-start.14 = (bf16[2,656,384]{2,1,0:T(8,128)(2,1)}, bf16[2,656,384]{2,1,0:T(8,128)(2,1)}, u32[]{:S(2)}, u32[]{:S(2)}) collective-permute-start(bf16[2,656,384]{2,1,0:T(8,128)(2,1)} %collective-permute-done.6.refs_4_.refs_1_), channel_id=1, source_target_pairs={{0,1},{1,0},{2,3},{3,2},{4,5},{5,4},{6,7},{7,6},{8,9},{9,8},{10,11... | collective-permute-start | bytes 3022856 | tf_op jit(solution)/shard_map/ppermute | solution.py:33
  122.9 18.8 %collective-permute-start.20 = (bf16[4,320,384]{2,1,0:T(8,128)(2,1)}, bf16[4,320,384]{2,1,0:T(8,128)(2,1)}, u32[]{:S(2)}, u32[]{:S(2)}) collective-permute-start(bf16[4,320,384]{2,1,0:T(8,128)(2,1)} %bitcast.17), channel_id=1, source_target_pairs={{0,1},{1,0},{2,3},{3,2},{4,5},{5,4},{6,7},{7,6},{8,9},{9,8},{10,11... | collective-permute-start | bytes 2949128 | tf_op jit(solution)/shard_map/ppermute | solution.py:33
  123.4 18.3 %collective-permute-start.24 = (bf16[4,320,384]{2,1,0:T(8,128)(2,1)}, bf16[4,320,384]{2,1,0:T(8,128)(2,1)}, u32[]{:S(2)}, u32[]{:S(2)}) collective-permute-start(bf16[4,320,384]{2,1,0:T(8,128)(2,1)} %bitcast.23), channel_id=1, source_target_pairs={{0,1},{1,0},{2,3},{3,2},{4,5},{5,4},{6,7},{7,6},{8,9},{9,8},{10,11... | collective-permute-start | bytes 2949128 | tf_op jit(solution)/shard_map/ppermute | solution.py:33
  123.4 18.3 %collective-permute-start.21 = (bf16[4,320,384]{2,1,0:T(8,128)(2,1)}, bf16[4,320,384]{2,1,0:T(8,128)(2,1)}, u32[]{:S(2)}, u32[]{:S(2)}) collective-permute-start(bf16[4,320,384]{2,1,0:T(8,128)(2,1)} %bitcast.19), channel_id=1, source_target_pairs={{0,1},{1,0},{2,3},{3,2},{4,5},{5,4},{6,7},{7,6},{8,9},{9,8},{10,11... | collective-permute-start | bytes 2949128 | tf_op jit(solution)/shard_map/ppermute | solution.py:33
  143.7 8.3 %collective-permute-start.28 = (bf16[2,320,384]{2,1,0:T(8,128)(2,1)S(1)}, bf16[2,320,384]{2,1,0:T(8,128)(2,1)S(1)}, u32[]{:S(2)}, u32[]{:S(2)}) collective-permute-start(bf16[2,320,384]{2,1,0:T(8,128)(2,1)S(1)} %get-tuple-element.38), channel_id=1, source_target_pairs={{0,24},{1,7},{2,26},{3,1},{4,28},{5,3},{6,30},{7,5},{8,0},{9,15},{... | collective-permute-start | bytes 1474568 | tf_op jit(solution)/shard_map/ppermute | solution.py:29
  144.1 9.2 %collective-permute-start.22 = (bf16[2,320,384]{2,1,0:T(8,128)(2,1)S(1)}, bf16[2,320,384]{2,1,0:T(8,128)(2,1)S(1)}, u32[]{:S(2)}, u32[]{:S(2)}) collective-permute-start(bf16[2,320,384]{2,1,0:T(8,128)(2,1)S(1)} %get-tuple-element.37), channel_id=1, source_target_pairs={{0,8},{1,3},{2,10},{3,5},{4,12},{5,7},{6,14},{7,1},{8,16},{9,11},{... | collective-permute-start | bytes 1474568 | tf_op jit(solution)/shard_map/ppermute | solution.py:29
  145.6 12.3 %copy-start.10 = (bf16[1,6144,256]{2,1,0:T(8,128)(2,1)S(1)}, bf16[1,6144,256]{2,1,0:T(8,128)(2,1)}, u32[]{:S(2)}) copy-start(bf16[1,6144,256]{2,1,0:T(8,128)(2,1)} %param.16) | copy-start | bytes 9437188
  145.6 14.8 %copy-start.38 = (bf16[2,656,384]{2,1,0:T(8,128)(2,1)S(1)}, bf16[2,656,384]{2,1,0:T(8,128)(2,1)}, u32[]{:S(2)}) copy-start(bf16[2,656,384]{2,1,0:T(8,128)(2,1)} %copy-done.36) | copy-start | bytes 3022852
  145.6 14.8 %copy-start.42 = (bf16[2,656,384]{2,1,0:T(8,128)(2,1)S(1)}, bf16[2,656,384]{2,1,0:T(8,128)(2,1)}, u32[]{:S(2)}) copy-start(bf16[2,656,384]{2,1,0:T(8,128)(2,1)} %copy-done.40) | copy-start | bytes 3022852
  145.6 14.9 %copy-start.50 = (f32[320,256]{1,0:T(8,128)S(1)}, f32[320,256]{1,0:T(8,128)}, u32[]{:S(2)}) copy-start(f32[320,256]{1,0:T(8,128)} %copy-done.49) | copy-start | bytes 983044
  145.6 14.9 %copy-start.52 = (f32[320,256]{1,0:T(8,128)S(1)}, f32[320,256]{1,0:T(8,128)}, u32[]{:S(2)}) copy-start(f32[320,256]{1,0:T(8,128)} %copy-done.51) | copy-start | bytes 983044
  145.6 14.9 %copy-start.54 = (bf16[320,256]{1,0:T(8,128)(2,1)S(1)}, bf16[320,256]{1,0:T(8,128)(2,1)}, u32[]{:S(2)}) copy-start(bf16[320,256]{1,0:T(8,128)(2,1)} %copy-done.53) | copy-start | bytes 491524
  147.0 10.9 %copy-start.7 = (bf16[1,6144,256]{2,1,0:T(8,128)(2,1)S(1)}, bf16[1,6144,256]{2,1,0:T(8,128)(2,1)}, u32[]{:S(2)}) copy-start(bf16[1,6144,256]{2,1,0:T(8,128)(2,1)} %param.15) | copy-start | bytes 9437188
  147.0 24.5 %collective-permute-start.19 = (bf16[4,320,384]{2,1,0:T(8,128)(2,1)S(1)}, bf16[4,320,384]{2,1,0:T(8,128)(2,1)S(1)}, u32[]{:S(2)}, u32[]{:S(2)}) collective-permute-start(bf16[4,320,384]{2,1,0:T(8,128)(2,1)S(1)} %bitcast.170), channel_id=1, source_target_pairs={{0,1},{1,0},{2,3},{3,2},{4,5},{5,4},{6,7},{7,6},{8,9},{9,8},{10,11... | collective-permute-start | bytes 2949128 | tf_op jit(solution)/shard_map/ppermute | solution.py:33
  147.3 24.1 %collective-permute-start.25 = (bf16[2,320,384]{2,1,0:T(8,128)(2,1)S(1)}, bf16[2,320,384]{2,1,0:T(8,128)(2,1)S(1)}, u32[]{:S(2)}, u32[]{:S(2)}) collective-permute-start(bf16[2,320,384]{2,1,0:T(8,128)(2,1)S(1)} %get-tuple-element.41), channel_id=1, source_target_pairs={{0,24},{1,7},{2,26},{3,1},{4,28},{5,3},{6,30},{7,5},{8,0},{9,15},{... | collective-permute-start | bytes 1474568 | tf_op jit(solution)/shard_map/ppermute | solution.py:29
  148.4 23.1 %collective-permute-start.27 = (bf16[2,320,384]{2,1,0:T(8,128)(2,1)S(1)}, bf16[2,320,384]{2,1,0:T(8,128)(2,1)S(1)}, u32[]{:S(2)}, u32[]{:S(2)}) collective-permute-start(bf16[2,320,384]{2,1,0:T(8,128)(2,1)S(1)} %get-tuple-element.42), channel_id=1, source_target_pairs={{0,8},{1,3},{2,10},{3,5},{4,12},{5,7},{6,14},{7,1},{8,16},{9,11},{... | collective-permute-start | bytes 1474568 | tf_op jit(solution)/shard_map/ppermute | solution.py:29
  153.3 7.1 %copy-start.35 = (bf16[2,656,384]{2,1,0:T(8,128)(2,1)S(1)}, bf16[2,656,384]{2,1,0:T(8,128)(2,1)}, u32[]{:S(2)}) copy-start(bf16[2,656,384]{2,1,0:T(8,128)(2,1)} %copy-done.33) | copy-start | bytes 3022852
  155.0 16.5 %collective-permute-start.23 = (bf16[2,320,384]{2,1,0:T(8,128)(2,1)S(1)}, bf16[2,320,384]{2,1,0:T(8,128)(2,1)S(1)}, u32[]{:S(2)}, u32[]{:S(2)}) collective-permute-start(bf16[2,320,384]{2,1,0:T(8,128)(2,1)S(1)} %get-tuple-element.39), channel_id=1, source_target_pairs={{0,8},{1,3},{2,10},{3,5},{4,12},{5,7},{6,14},{7,1},{8,16},{9,11},{... | collective-permute-start | bytes 1474568 | tf_op jit(solution)/shard_map/ppermute | solution.py:29
  155.3 16.2 %collective-permute-start.29 = (bf16[2,320,384]{2,1,0:T(8,128)(2,1)S(1)}, bf16[2,320,384]{2,1,0:T(8,128)(2,1)S(1)}, u32[]{:S(2)}, u32[]{:S(2)}) collective-permute-start(bf16[2,320,384]{2,1,0:T(8,128)(2,1)S(1)} %get-tuple-element.40), channel_id=1, source_target_pairs={{0,24},{1,7},{2,26},{3,1},{4,28},{5,3},{6,30},{7,5},{8,0},{9,15},{... | collective-permute-start | bytes 1474568 | tf_op jit(solution)/shard_map/ppermute | solution.py:29
  160.4 22.2 %copy-start.1 = (bf16[256,6144]{1,0:T(8,128)(2,1)}, bf16[256,6144]{1,0:T(8,128)(2,1)S(1)}, u32[]{:S(2)}) copy-start(bf16[256,6144]{1,0:T(8,128)(2,1)S(1)} %get-tuple-element.28.refs_9_.refs_10_.refs_11_.refs_12_.refs_8_) | copy-start | bytes 9437188
  160.4 22.2 %copy-start.3 = (bf16[256,6144]{1,0:T(8,128)(2,1)}, bf16[256,6144]{1,0:T(8,128)(2,1)S(1)}, u32[]{:S(2)}) copy-start(bf16[256,6144]{1,0:T(8,128)(2,1)S(1)} %get-tuple-element.29.refs_11_.refs_12_.refs_13_.refs_14_.refs_10_) | copy-start | bytes 9437188
  171.4 11.2 %copy-start.43 = (bf16[512,640]{1,0:T(8,128)(2,1)}, bf16[512,640]{1,0:T(8,128)(2,1)S(1)}, u32[]{:S(2)}) copy-start(bf16[512,640]{1,0:T(8,128)(2,1)S(1)} %get-tuple-element.26.left_ref) | copy-start | bytes 1966084
  171.9 19.4 %collective-permute-start.26 = (bf16[320,384]{1,0:T(8,128)(2,1)S(1)}, bf16[320,384]{1,0:T(8,128)(2,1)S(1)}, u32[]{:S(2)}, u32[]{:S(2)}) collective-permute-start(bf16[320,384]{1,0:T(8,128)(2,1)S(1)} %get-tuple-element.36), channel_id=1, source_target_pairs={{0,2},{1,9},{2,4},{3,11},{4,6},{5,13},{6,0},{7,15},{8,10},{9,17},{... | collective-permute-start | bytes 737288 | tf_op jit(solution)/shard_map/ppermute | solution.py:29
  172.0 19.3 %collective-permute-start.30 = (bf16[320,384]{1,0:T(8,128)(2,1)S(1)}, bf16[320,384]{1,0:T(8,128)(2,1)S(1)}, u32[]{:S(2)}, u32[]{:S(2)}) collective-permute-start(bf16[320,384]{1,0:T(8,128)(2,1)S(1)} %get-tuple-element.34), channel_id=1, source_target_pairs={{0,4},{1,17},{2,6},{3,19},{4,0},{5,21},{6,2},{7,23},{8,12},{9,25},... | collective-permute-start | bytes 737288 | tf_op jit(solution)/shard_map/ppermute | solution.py:29
  173.6 17.7 %collective-permute-start.31 = (bf16[320,384]{1,0:T(8,128)(2,1)S(1)}, bf16[320,384]{1,0:T(8,128)(2,1)S(1)}, u32[]{:S(2)}, u32[]{:S(2)}) collective-permute-start(bf16[320,384]{1,0:T(8,128)(2,1)S(1)} %get-tuple-element.35), channel_id=1, source_target_pairs={{0,6},{1,25},{2,0},{3,27},{4,2},{5,29},{6,4},{7,31},{8,14},{9,1},{... | collective-permute-start | bytes 737288 | tf_op jit(solution)/shard_map/ppermute | solution.py:29
  192.2 21.8 %all-to-all-start.2 = ((bf16[8,40,384]{2,1,0:T(8,128)(2,1)}), bf16[8,40,384]{2,1,0:T(8,128)(2,1)}, u32[]{:S(2)}, u32[]{:S(2)}) async-start(bf16[8,40,384]{2,1,0:T(8,128)(2,1)} %bitcast.171), calls=%async_computation.2 | async-start | bytes 491520 | tf_op jit(solution)/shard_map/all_to_all | solution.py:453
  (43 other events, 98.8 us)
where the time goes:
time: 219 us; the launch traced here: 216 us
  Pallas kernels  58.2 us (27%)
  starting transfers between devices  45.5 us (21%)
  local copies, waits for them, and re-layouts  39.3 us (18%)
  blocking collectives  34.1 us (16%)
  waiting for transfers between devices  24.3 us (11%)
  other arithmetic  9.99 us (5%)
  matrix products  3.46 us (2%)
    unnamed x117, local copies, waits for them, and re-layouts  37.8 us
    all_to_all x1, blocking collectives, to_experts(): return lax.all_to_all(block, 'tok', split_axis=0, concat_axis=0, tiled=True)  25.2 us
    ppermute x18, waiting for transfers between devices, plane_shift(): return lax.ppermute(value, ('tp', 'grp'), pairs)  22.6 us
    pallas_call x3, Pallas kernels, score(): pl.pallas_call(functools.partial(score_body, rows, start, steps), out_sha...  22.1 us
    ppermute x18, starting transfers between devices, plane_shift(): return lax.ppermute(value, ('tp', 'grp'), pairs)  20.9 us
    ppermute x14, starting transfers between devices, swap_cores(): return lax.ppermute(value, 'grp', [(0, 1), (1, 0)])  20.6 us
    pallas_call x5, Pallas kernels, down(): pl.pallas_call(down_body, out_shape=jax.ShapeDtypeStruct((count, 4, rows,...  11.7 us
    pallas_call x2, Pallas kernels, forward(): pl.pallas_call(functools.partial(forward_body, rows, width), out_shape=(n...  11 us
  transfers between devices with their start and end apart: 33, of which 9 were waited for; matrix products, arithmetic and copies ran while one was open for 2% of the time, Pallas kernels for 21%

commit v1 on v0

--- a/solution.py
+++ b/solution.py
@@ -11,7 +11,9 @@
 
 GAIN_ROWS = 16
 VMEM_LIMIT = 16 << 20
-SCORE_STEPS = ((0, 3), (3, 3), (6, 2))
+EARLY = (0, 1, 6, 3)
+LATE = (2, 7, 4, 5)
+SCORE_STEPS = ((0, 3), (3, 4), (7, 1))
 
 
 def plane_shift(value, stage, step):
@@ -137,9 +139,9 @@
         activated = gate_pre * sigmoid_gate
         act = (activated * up_proj).astype(jnp.bfloat16)
         act_ref[...] = act
-        left_ref[...] = (act.astype(jnp.float32) * scale_ref[...]).astype(jnp.bfloat16)
+        left_ref[...] = (act.astype(jnp.float32) * scale_ref[:, :1]).astype(jnp.bfloat16)
         slope = up_proj * sigmoid_gate * (1.0 + gate_pre * (1.0 - sigmoid_gate))
-        scaling = scaling * scale_ref[...]
+        scaling = scaling * scale_ref[:, :1]
         slope_ref[...] = slope * scaling
         lin_ref[...] = activated * scaling
 
@@ -163,7 +165,7 @@
             in_specs=[pl.BlockSpec(memory_space=pl.ANY)] * 8
             + row_specs
             + row_specs
-            + [pl.BlockSpec((rows, 1), lambda s, t: (0, 0))],
+            + [pl.BlockSpec((rows, 128), lambda s, t: (0, 0))],
             out_specs=[whole, whole, whole, whole],
             scratch_shapes=[
                 pltpu.VMEM((rows, units), jnp.float32),
@@ -214,10 +216,13 @@
     )(table, act, down_mat, down_mat)
 
 
-def grads_body(rows, table, other_table, *refs):
-    pieces, own_refs, other_refs = refs[0:16], refs[16:18], refs[18:20]
-    act_o, act_p, slope_o, slope_p, lin_o, lin_p = refs[20:26]
-    left_ref, acts_ref, grad_acc, held, sems = refs[26:]
+def part_of(table, numbers):
+    return jnp.concatenate([table[2 * number : 2 * number + 2] for number in numbers])
+
+
+def grads_step(rows, count, refs, grad_acc, held, sems):
+    pieces = refs[0 : 2 * count]
+    own_refs, other_refs = refs[2 * count : 2 * count + 2], refs[2 * count + 2 : 2 * count + 4]
     step = pl.program_id(0)
 
     def copy(piece, at):
@@ -226,22 +231,45 @@
 
     @pl.when(step == 0)
     def _():
-        for at in range(8):
+        for at in range(count):
             copy(pieces[at], at).start()
-            copy(pieces[at + 8], at + 8).start()
-        grad_acc[...] = jnp.zeros_like(grad_acc)
+            copy(pieces[at + count], at + count).start()
 
     dims = (((1,), (1,)), ((), ()))
     copy(pieces[0], step).wait()
     cot = jnp.concatenate([held[step, j] for j in range(2)], axis=1)
     mat = jnp.concatenate([r[...] for r in own_refs], axis=1)
     grad_acc[:rows, :] += lax.dot_general(cot, mat, dims, preferred_element_type=jnp.float32)
-    copy(pieces[0], step + 8).wait()
-    cot = jnp.concatenate([held[step + 8, j] for j in range(2)], axis=1)
+    copy(pieces[0], step + count).wait()
+    cot = jnp.concatenate([held[step + count, j] for j in range(2)], axis=1)
     mat = jnp.concatenate([r[...] for r in other_refs], axis=1)
     grad_acc[rows:, :] += lax.dot_general(cot, mat, dims, preferred_element_type=jnp.float32)
 
-    @pl.when(step == 7)
+
+def grads_early(rows, count, table, other_table, *refs):
+    grad_acc, held, sems = refs[-3:]
+
+    @pl.when(pl.program_id(0) == 0)
+    def _():
+        grad_acc[...] = jnp.zeros_like(grad_acc)
+
+    grads_step(rows, count, refs, grad_acc, held, sems)
+
+
+def grads_late(rows, count, table, other_table, *refs):
+    before, act_o, act_p, slope_o, slope_p, lin_o, lin_p, left_ref, acts_ref = refs[
+        2 * count + 4 : 2 * count + 13
+    ]
+    grad_acc, held, sems = refs[-3:]
+    step = pl.program_id(0)
+
+    @pl.when(step == 0)
+    def _():
+        grad_acc[...] = before[...]
+
+    grads_step(rows, count, refs, grad_acc, held, sems)
+
+    @pl.when(step == count - 1)
     def _():
         units = grad_acc.shape[1]
         grad = grad_acc[...]
@@ -253,44 +281,62 @@
         acts_ref[...] = act.T.astype(jnp.bfloat16)
 
 
-def activation_grads(tables, pieces, down_mat, saved):
-    rows = saved[0].shape[0]
-    slice_width = pieces[0].shape[2]
+def activation_grads(tables, own, other, numbers, down_mat, before=None, saved=None):
+    slice_width = own[0].shape[2]
+    rows = (own[0].shape[1] - GAIN_ROWS) // 2
     units, width = down_mat.shape
+    count = len(numbers)
     whole = pl.BlockSpec((rows, units), lambda s, *t: (0, 0))
+    double = pl.BlockSpec((2 * rows, units), lambda s, *t: (0, 0))
 
     def at(s):
         return s
 
-    return pl.pallas_call(
-        functools.partial(grads_body, rows),
-        out_shape=(
+    in_specs = (
+        [pl.BlockSpec(memory_space=pl.ANY)] * (2 * count)
+        + column_specs(units, slice_width, at, 0)
+        + column_specs(units, slice_width, at, 1)
+    )
+    operands = [side[number] for side in (own, other) for number in numbers] + [down_mat] * 4
+    scratch = [
+        pltpu.VMEM((2 * count, 2, rows, slice_width), jnp.bfloat16),
+        pltpu.SemaphoreType.DMA((2 * count,)),
+    ]
+    if saved is None:
+        body = functools.partial(grads_early, rows, count)
+        out_shape = jax.ShapeDtypeStruct((2 * rows, units), jnp.float32)
+        out_specs = double
+    else:
+        body = functools.partial(grads_late, rows, count)
+        out_shape = (
             jax.ShapeDtypeStruct((2 * units, 2 * rows), jnp.bfloat16),
             jax.ShapeDtypeStruct((units, 2 * rows), jnp.bfloat16),
-        ),
+        )
+        out_specs = [
+            pl.BlockSpec((2 * units, 2 * rows), lambda s, *t: (0, 0)),
+            pl.BlockSpec((units, 2 * rows), lambda s, *t: (0, 0)),
+        ]
+        in_specs = in_specs + [double] + [whole] * 6
+        operands += [before, *saved]
+        scratch = [pltpu.VMEM((2 * rows, units), jnp.float32)] + scratch
+    return pl.pallas_call(
+        body,
+        out_shape=out_shape,
         grid_spec=pltpu.PrefetchScalarGridSpec(
             num_scalar_prefetch=2,
-            grid=(8,),
-            in_specs=[pl.BlockSpec(memory_space=pl.ANY)] * 16
-            + column_specs(units, slice_width, at, 0)
-            + column_specs(units, slice_width, at, 1)
-            + [whole] * 6,
-            out_specs=[
-                pl.BlockSpec((2 * units, 2 * rows), lambda s, *t: (0, 0)),
-                pl.BlockSpec((units, 2 * rows), lambda s, *t: (0, 0)),
-            ],
-            scratch_shapes=[
-                pltpu.VMEM((2 * rows, units), jnp.float32),
-                pltpu.VMEM((16, 2, rows, slice_width), jnp.bfloat16),
-                pltpu.SemaphoreType.DMA((16,)),
-            ],
-        ),
-        compiler_params=pltpu.CompilerParams(vmem_limit_bytes=VMEM_LIMIT + (4 << 20)),
+            grid=(count,),
+            in_specs=in_specs,
+            out_specs=out_specs,
+            scratch_shapes=scratch,
+        ),
+        compiler_params=pltpu.CompilerParams(vmem_limit_bytes=VMEM_LIMIT),
         cost_estimate=pl.CostEstimate(
-            flops=4 * rows * width * units, transcendentals=0, bytes_accessed=14 << 20
+            flops=count * rows * width * units // 2,
+            transcendentals=0,
+            bytes_accessed=count * (7 << 18),
         ),
         name="grads",
-    )(*tables, *pieces, *([down_mat] * 4), *saved)
+    )(*(part_of(table, numbers) for table in tables), *operands)
 
 
 def score_body(rows, start, steps, table, left_ref, acts_ref, *refs):
@@ -478,14 +524,20 @@
     matches = matches_of(capacity)
     slot_scale = jnp.sum(jnp.where(matches, scaled[None, :, :], 0.0), axis=(1, 2))
     combining = jnp.sum(jnp.where(matches, gate_weights[None, :, :], 0.0), axis=2)
+    wide_scale = jnp.broadcast_to(slot_scale[:, None], (experts * capacity, 128))
     scale_own = lax.all_to_all(
-        slot_scale.reshape(experts, capacity), "tok", split_axis=0, concat_axis=0, tiled=True
-    )
-    scale_other = swap_cores(scale_own).reshape(-1, 1)
-    scale_own = scale_own.reshape(-1, 1)
+        wide_scale.reshape(experts, capacity, 128),
+        "tok",
+        split_axis=0,
+        concat_axis=0,
+        tiled=True,
+    ).reshape(experts * capacity, 128)
+    scale_other = swap_cores(scale_own)
 
     gate_mat, up_mat, down_mat = w_gate[0], w_up[0], w_down[0]
     gate_cols, up_cols = turned(gate_mat, up_mat)
+    tables = (table, other_table)
+    sums_grad = activation_grads(tables, own_pieces, other_pieces, EARLY, down_mat)
     act_own, left_own, slope_own, lin_own = forward(own_pieces, table, gate_mat, up_mat, scale_own)
     part_own = down(act_own, table, 0, 4, down_mat)
     act_other, left_other, slope_other, lin_other = forward(
@@ -499,7 +551,7 @@
 
     saved = (left_own, left_other, slope_own, slope_other, lin_own, lin_other)
     lefts = activation_grads(
-        (table, other_table), own_pieces + other_pieces, down_mat, saved
+        tables, own_pieces, other_pieces, LATE, down_mat, sums_grad, saved
     )
     scores = 0.0
     for start, steps in SCORE_STEPS:

time: 219 us -> 207 us (0.945)
  local copies, waits for them, and re-layouts: 39.3 us -> 26.9 us
  other arithmetic: 9.99 us -> 6.81 us
  waiting for transfers between devices: 24.3 us -> 26.8 us
  blocking collectives: 34.1 us -> 36.4 us
    unnamed x117 -> x85, local copies, waits for them, and re-layouts: 37.8 us -> 25.7 us
    ppermute x14, starting transfers between devices: 20.6 us -> 16.6 us  [swap_cores(): return lax.ppermute(value, 'grp', [(0, 1), (1, 0)])]
    ppermute x18, starting transfers between devices: 20.9 us -> 24.5 us  [plane_shift(): return lax.ppermute(value, ('tp', 'grp'), pairs)]
    convert_element_type x4, other arithmetic: 4.99 us -> 2.32 us  [add_wide(): return total.astype(jnp.bfloat16)]
    pallas_call x5, Pallas kernels: 11.7 us -> 9.27 us  [down(): pl.pallas_call(down_body, out_shape=jax.ShapeDtypeStruct((count, 4, rows,...]
    all_to_all x1, blocking collectives: 8.92 us -> 11.3 us  [on_device(): lax.all_to_all(wide_scale.reshape(experts, capacity, 128), 'tok', split_a...]
    pallas_call x1 -> x2, Pallas kernels: 10.9 us -> 13 us  [activation_grads(): pl.pallas_call(body, out_shape=out_shape, grid_spec=pltpu.PrefetchScalarG...]
  transfers between devices with their start and end apart: 33 -> 33, of which waited for: 9 -> 8; matrix products, arithmetic and copies ran while one was open for 2% -> 1% of each run, Pallas kernels for 21% -> 23%
where the time goes in v1:
time: 207 us; the launch traced here: 205 us
  Pallas kernels  57.7 us (28%)
  starting transfers between devices  45.1 us (22%)
  blocking collectives  36.4 us (18%)
  local copies, waits for them, and re-layouts  26.9 us (13%)
  waiting for transfers between devices  26.8 us (13%)
  other arithmetic  6.81 us (3%)
  matrix products  3.46 us (2%)
    unnamed x85, local copies, waits for them, and re-layouts  25.7 us
    all_to_all x1, blocking collectives, to_experts(): return lax.all_to_all(block, 'tok', split_axis=0, concat_axis=0, tiled=True)  25.1 us
    ppermute x18, starting transfers between devices, plane_shift(): return lax.ppermute(value, ('tp', 'grp'), pairs)  24.5 us
    ppermute x18, waiting for transfers between devices, plane_shift(): return lax.ppermute(value, ('tp', 'grp'), pairs)  24.4 us
    pallas_call x3, Pallas kernels, score(): pl.pallas_call(functools.partial(score_body, rows, start, steps), out_sha...  21.9 us
    ppermute x14, starting transfers between devices, swap_cores(): return lax.ppermute(value, 'grp', [(0, 1), (1, 0)])  16.6 us
    pallas_call x2, Pallas kernels, activation_grads(): pl.pallas_call(body, out_shape=out_shape, grid_spec=pltpu.PrefetchScalarG...  13 us
    all_to_all x1, blocking collectives, on_device(): lax.all_to_all(wide_scale.reshape(experts, capacity, 128), 'tok', split_a...  11.3 us
  transfers between devices with their start and end apart: 33, of which 8 were waited for; matrix products, arithmetic and copies ran while one was open for 1% of the time, Pallas kernels for 23%

profile of v1, /device:TPU:1, one launch (start us, length us, event | category | flops | bytes accessed | tf_op | source)
XLA Modules:
  0.0 204.6 jit_solution(2326271311946854788)
XLA Ops:
  4.7 1.3 fusion.1
  6.0 25.1 %all_to_all.15 = bf16[8,88,384]{2,1,0:T(8,128)(2,1)S(1)} all-to-all(bf16[8,88,384]{2,1,0:T(8,128)(2,1)S(1)} %bitcast.183), channel_id=1, replica_groups=mesh['tok'=8,'tp'=16,'grp'=2] {'tok'}, dimensions={0} | all-to-all | bytes 1081344 | tf_op jit(solution)/shard_map/all_to_all | solution.py:499
  31.3 3.0 %collective-permute-start.1 = (bf16[656,384]{1,0:T(8,128)(2,1)S(1)}, bf16[656,384]{1,0:T(8,128)(2,1)S(1)}, u32[]{:S(2)}, u32[]{:S(2)}) collective-permute-start(bf16[656,384]{1,0:T(8,128)(2,1)S(1)} %get-tuple-element.46), channel_id=1, source_target_pairs={{0,4},{1,17},{2,6},{3,19},{4,0},{5,21},{6,2},{7,23},{8,12},{9,25},... | collective-permute-start | bytes 1511432 | tf_op jit(solution)/shard_map/ppermute | solution.py:31
  34.7 2.3 %collective-permute-start = (bf16[656,384]{1,0:T(8,128)(2,1)S(1)}, bf16[656,384]{1,0:T(8,128)(2,1)S(1)}, u32[]{:S(2)}, u32[]{:S(2)}) collective-permute-start(bf16[656,384]{1,0:T(8,128)(2,1)S(1)} %get-tuple-element.46), channel_id=1, source_target_pairs={{0,6},{1,25},{2,0},{3,27},{4,2},{5,29},{6,4},{7,31},{8,14},{9,1},{... | collective-permute-start | bytes 1511432 | tf_op jit(solution)/shard_map/ppermute | solution.py:31
  37.0 3.2 %collective-permute-start.9 = (f32[16]{0:T(128)S(1)}, f32[16]{0:T(128)S(1)}, u32[]{:S(2)}, u32[]{:S(2)}) collective-permute-start(f32[16]{0:T(128)S(1)} %fusion.22), channel_id=1, source_target_pairs={{0,1},{1,0},{2,3},{3,2},{4,5},{5,4},{6,7},{7,6},{8,9},{9,8},{10,11... | collective-permute-start | bytes 200 | tf_op jit(solution)/shard_map/ppermute | solution.py:35
  41.1 5.3 %collective-permute-done.2 = bf16[656,384]{1,0:T(8,128)(2,1)S(1)} collective-permute-done((bf16[656,384]{1,0:T(8,128)(2,1)S(1)}, bf16[656,384]{1,0:T(8,128)(2,1)S(1)}, u32[]{:S(2)}, u32[]{:S(2)}) %collective-permute-start.2) | collective-permute-done | bytes 503840 | tf_op jit(solution)/shard_map/ppermute | solution.py:31
  46.5 2.6 %collective-permute-start.4 = (bf16[2,656,384]{2,1,0:T(8,128)(2,1)S(1)}, bf16[2,656,384]{2,1,0:T(8,128)(2,1)}, u32[]{:S(2)}, u32[]{:S(2)}) collective-permute-start(bf16[2,656,384]{2,1,0:T(8,128)(2,1)S(1)} %pad_maximum_fusion.1.refs_1_), channel_id=1, source_target_pairs={{0,24},{1,7},{2,26},{3,1},{4,28},{5,3},{6,30},{7,5},{8,0},{9,15},{... | collective-permute-start | bytes 3022856 | tf_op jit(solution)/shard_map/ppermute | solution.py:31
  49.1 3.8 %collective-permute-start.11 = (bf16[2,656,384]{2,1,0:T(8,128)(2,1)S(1)}, bf16[2,656,384]{2,1,0:T(8,128)(2,1)S(1)}, u32[]{:S(2)}, u32[]{:S(2)}) collective-permute-start(bf16[2,656,384]{2,1,0:T(8,128)(2,1)S(1)} %pad_maximum_fusion.1.refs_1_), channel_id=1, source_target_pairs={{0,1},{1,0},{2,3},{3,2},{4,5},{5,4},{6,7},{7,6},{8,9},{9,8},{10,11... | collective-permute-start | bytes 3022856 | tf_op jit(solution)/shard_map/ppermute | solution.py:35
  53.0 1.4 collective-permute-start.5
  55.3 11.3 %all_to_all.16 = f32[8,40,128]{2,1,0:T(8,128)S(1)} all-to-all(f32[8,40,128]{2,1,0:T(8,128)S(1)} %broadcast_in_dim.74), channel_id=1, replica_groups=mesh['tok'=8,'tp'=16,'grp'=2] {'tok'}, dimensions={0} | all-to-all | bytes 327680 | tf_op jit(solution)/shard_map/all_to_all | solution.py:528
  66.6 1.8 collective-permute-start.18
  69.7 2.4 %collective-permute-start.3 = (bf16[2,656,384]{2,1,0:T(8,128)(2,1)S(1)}, bf16[2,656,384]{2,1,0:T(8,128)(2,1)}, u32[]{:S(2)}, u32[]{:S(2)}) collective-permute-start(bf16[2,656,384]{2,1,0:T(8,128)(2,1)S(1)} %pad_maximum_fusion.refs_0_), channel_id=1, source_target_pairs={{0,24},{1,7},{2,26},{3,1},{4,28},{5,3},{6,30},{7,5},{8,0},{9,15},{... | collective-permute-start | bytes 3022856 | tf_op jit(solution)/shard_map/ppermute | solution.py:31
  75.0 1.4 collective-permute-start.7
  76.5 7.8 %collective-permute-done.8.refs_7_.refs_1_.refs_0_ = bf16[2,656,384]{2,1,0:T(8,128)(2,1)} collective-permute-done((bf16[2,656,384]{2,1,0:T(8,128)(2,1)S(1)}, bf16[2,656,384]{2,1,0:T(8,128)(2,1)}, u32[]{:S(2)}, u32[]{:S(2)}) %collective-permute-start.8) | collective-permute-done | bytes 1007648 | tf_op jit(solution)/shard_map/ppermute | solution.py:31
  84.3 1.2 collective-permute-start.16
  87.0 7.3 %collective-permute-done.7.refs_5_.refs_3_.refs_2_ = bf16[2,656,384]{2,1,0:T(8,128)(2,1)} collective-permute-done((bf16[2,656,384]{2,1,0:T(8,128)(2,1)}, bf16[2,656,384]{2,1,0:T(8,128)(2,1)}, u32[]{:S(2)}, u32[]{:S(2)}) %collective-permute-start.7) | collective-permute-done | bytes 1007648 | tf_op jit(solution)/shard_map/ppermute | solution.py:31
  94.4 1.5 collective-permute-start.15
  99.9 1.9 copy-done.7
  101.8 1.9 copy-done.9
  103.6 1.2 copy-done.12
  104.9 1.2 copy-done.16
  106.1 1.2 copy-done.26
  107.3 1.2 copy-done.30
  108.5 1.2 copy-done.33
  109.7 5.9 %forward.3 = (bf16[320,256]{1,0:T(8,128)(2,1)S(1)}, bf16[320,256]{1,0:T(8,128)(2,1)S(1)}, f32[320,256]{1,0:T(8,128)S(1)}, f32[320,256]{1,0:T(8,128)S(1)}) custom-call(s32[16]{0:T(128)S(1)} %fusion.27.table, bf16[2,656,384]{2,1,0:T(8,128)(2,1)} %collective-permute-done.10.refs_0_.refs_4_.refs_3_, bf16[2,656,384]{2,1,0:T(8,128)(2,1)S(1)} %copy-done.30, ...), custom_call_target="tpu_custom_call" | custom-call | flops 2013265920 | bytes 11534336 | tf_op jit(solution)/shard_map/forward/pallas_call | solution.py:159
  115.6 1.4 down.7
  117.0 1.4 down.9
  118.4 1.4 down.8
  121.5 5.1 %forward.2 = (bf16[320,256]{1,0:T(8,128)(2,1)S(1)}, bf16[320,256]{1,0:T(8,128)(2,1)S(1)}, f32[320,256]{1,0:T(8,128)S(1)}, f32[320,256]{1,0:T(8,128)S(1)}) custom-call(s32[16]{0:T(128)S(1)} %fusion.26.table, bf16[2,656,384]{2,1,0:T(8,128)(2,1)S(1)} %copy-done.23, bf16[2,656,384]{2,1,0:T(8,128)(2,1)S(1)} %copy-done.20, ...), custom_call_target="tpu_custom_call" | custom-call | flops 2013265920 | bytes 11534336 | tf_op jit(solution)/shard_map/forward/pallas_call | solution.py:159
  126.6 3.8 %down.5 = bf16[4,4,320,384]{3,2,1,0:T(8,128)(2,1)S(1)} custom-call(s32[16]{0:T(128)S(1)} %fusion.26.table, bf16[320,256]{1,0:T(8,128)(2,1)S(1)} %get-tuple-element.16.act_ref, bf16[256,6144]{1,0:T(8,128)(2,1)S(1)} %bitcast.146, bf16[256,6144]{1,0:T(8,128)(2,1)S(1)} %bitcast.147), custom_call_target="tpu_custom_call" | custom-call | flops 1006632960 | bytes 8388608 | tf_op jit(solution)/shard_map/down/pallas_call | solution.py:199
  131.0 2.1 %collective-permute-start.28 = (bf16[2,320,384]{2,1,0:T(8,128)(2,1)S(1)}, bf16[2,320,384]{2,1,0:T(8,128)(2,1)S(1)}, u32[]{:S(2)}, u32[]{:S(2)}) collective-permute-start(bf16[2,320,384]{2,1,0:T(8,128)(2,1)S(1)} %get-tuple-element.38), channel_id=1, source_target_pairs={{0,24},{1,7},{2,26},{3,1},{4,28},{5,3},{6,30},{7,5},{8,0},{9,15},{... | collective-permute-start | bytes 1474568 | tf_op jit(solution)/shard_map/ppermute | solution.py:31
  133.2 1.4 down.6
  134.6 2.2 %collective-permute-start.19 = (bf16[4,320,384]{2,1,0:T(8,128)(2,1)S(1)}, bf16[4,320,384]{2,1,0:T(8,128)(2,1)S(1)}, u32[]{:S(2)}, u32[]{:S(2)}) collective-permute-start(bf16[4,320,384]{2,1,0:T(8,128)(2,1)S(1)} %bitcast.174), channel_id=1, source_target_pairs={{0,1},{1,0},{2,3},{3,2},{4,5},{5,4},{6,7},{7,6},{8,9},{9,8},{10,11... | collective-permute-start | bytes 2949128 | tf_op jit(solution)/shard_map/ppermute | solution.py:35
  136.8 1.4 collective-permute-start.25
  139.0 3.2 %collective-permute-done.22 = bf16[2,320,384]{2,1,0:T(8,128)(2,1)S(1)} collective-permute-done((bf16[2,320,384]{2,1,0:T(8,128)(2,1)S(1)}, bf16[2,320,384]{2,1,0:T(8,128)(2,1)S(1)}, u32[]{:S(2)}, u32[]{:S(2)}) %collective-permute-start.22) | collective-permute-done | bytes 491552 | tf_op jit(solution)/shard_map/ppermute | solution.py:31
  143.0 2.7 %collective-permute-start.29 = (bf16[2,320,384]{2,1,0:T(8,128)(2,1)S(1)}, bf16[2,320,384]{2,1,0:T(8,128)(2,1)S(1)}, u32[]{:S(2)}, u32[]{:S(2)}) collective-permute-start(bf16[2,320,384]{2,1,0:T(8,128)(2,1)S(1)} %get-tuple-element.40), channel_id=1, source_target_pairs={{0,24},{1,7},{2,26},{3,1},{4,28},{5,3},{6,30},{7,5},{8,0},{9,15},{... | collective-permute-start | bytes 1474568 | tf_op jit(solution)/shard_map/ppermute | solution.py:31
  145.7 2.5 %turn.1 = (bf16[256,6144]{1,0:T(8,128)(2,1)S(1)}, bf16[256,6144]{1,0:T(8,128)(2,1)S(1)}) custom-call(bf16[6144,256]{1,0:T(8,128)(2,1)S(1)} %bitcast.168, bf16[6144,256]{1,0:T(8,128)(2,1)S(1)} %bitcast.173), custom_call_target="tpu_custom_call" | custom-call | bytes 12582912 | tf_op jit(solution)/shard_map/turn/pallas_call | solution.py:453
  148.4 6.9 %grads.2.refs_12_ = f32[640,256]{1,0:T(8,128)S(1)} custom-call(s32[8]{0:T(128)S(1)} %get-tuple-element.60.table, s32[8]{0:T(128)S(1)} %get-tuple-element.61.other_table, bf16[2,656,384]{2,1,0:T(8,128)(2,1)S(1)} %copy-done.23, bf16[2,656,384]{2,1,0:T(8,128)(2,1)S(1)} %copy-done.20, bf16[2,656,384]{2,1,0:T(8,128)(2,1)} %collective-permute-done.5.refs_6_.refs_2_.refs_3_, ...), custom_call_target="tpu_custom_call" | custom-call | flops 1006632960 | bytes 7340032 | tf_op jit(solution)/shard_map/grads/pallas_call | solution.py:322
  155.4 6.1 %grads.3 = (bf16[512,640]{1,0:T(8,128)(2,1)S(1)}, bf16[256,640]{1,0:T(8,128)(2,1)S(1)}) custom-call(s32[8]{0:T(128)S(1)} %get-tuple-element.62.table, s32[8]{0:T(128)S(1)} %get-tuple-element.63.other_table, bf16[2,656,384]{2,1,0:T(8,128)(2,1)} %collective-permute-done.3.refs_2_.refs_0_, bf16[2,656,384]{2,1,0:T(8,128)(2,1)} %collective-permute-done.8.refs_7_.refs_1_.refs_0_, ...), custom_call_target="tpu_custom_call" | custom-call | flops 1006632960 | bytes 7340032 | tf_op jit(solution)/shard_map/grads/pallas_call | solution.py:322
  162.2 3.7 %collective-permute-start.30 = (bf16[320,384]{1,0:T(8,128)(2,1)S(1)}, bf16[320,384]{1,0:T(8,128)(2,1)S(1)}, u32[]{:S(2)}, u32[]{:S(2)}) collective-permute-start(bf16[320,384]{1,0:T(8,128)(2,1)S(1)} %get-tuple-element.34), channel_id=1, source_target_pairs={{0,4},{1,17},{2,6},{3,19},{4,0},{5,21},{6,2},{7,23},{8,12},{9,25},... | collective-permute-start | bytes 737288 | tf_op jit(solution)/shard_map/ppermute | solution.py:31
  166.1 10.6 %score.4 = f32[256,128]{1,0:T(8,128)S(1)} custom-call(s32[16]{0:T(128)S(1)} %fusion.26.table, bf16[512,640]{1,0:T(8,128)(2,1)S(1)} %get-tuple-element.26.left_ref, bf16[256,640]{1,0:T(8,128)(2,1)S(1)} %get-tuple-element.27.acts_ref, bf16[2,656,384]{2,1,0:T(8,128)(2,1)} %collective-permute-done.4.refs_3_.refs_0_, ...), custom_call_target="tpu_custom_call" | custom-call | flops 3019898880 | bytes 10485760 | tf_op jit(solution)/shard_map/score/pallas_call | solution.py:403
  177.7 4.0 %all-to-all-start.2 = ((bf16[8,40,384]{2,1,0:T(8,128)(2,1)}), bf16[8,40,384]{2,1,0:T(8,128)(2,1)}, u32[]{:S(2)}, u32[]{:S(2)}) async-start(bf16[8,40,384]{2,1,0:T(8,128)(2,1)} %bitcast.180), calls=%async_computation.2 | async-start | bytes 491520 | tf_op jit(solution)/shard_map/all_to_all | solution.py:499
  181.7 1.9 copy-done.2
  183.6 1.9 copy-done.5
  185.5 1.2 copy-done.21
  190.2 8.0 %score.3 = f32[256,128]{1,0:T(8,128)S(1)} custom-call(s32[16]{0:T(128)S(1)} %fusion.26.table, bf16[512,640]{1,0:T(8,128)(2,1)S(1)} %copy-done.36, bf16[256,640]{1,0:T(8,128)(2,1)S(1)} %get-tuple-element.27.acts_ref, bf16[2,656,384]{2,1,0:T(8,128)(2,1)S(1)} %copy-done.24, bf16[2,656,384]{2,1,0:T(8,128)(2,1)S(1)} %copy-done.21, ...), custom_call_target="tpu_custom_call" | custom-call | flops 2264924160 | bytes 7864320 | tf_op jit(solution)/shard_map/score/pallas_call | solution.py:403
  198.3 3.4 %score.5 = f32[256,128]{1,0:T(8,128)S(1)} custom-call(s32[16]{0:T(128)S(1)} %fusion.26.table, bf16[512,640]{1,0:T(8,128)(2,1)S(1)} %copy-done.36, bf16[256,640]{1,0:T(8,128)(2,1)S(1)} %get-tuple-element.27.acts_ref, bf16[2,656,384]{2,1,0:T(8,128)(2,1)} %collective-permute-done.8.refs_7_.refs_1_.refs_0_, bf16[2,656,384]{2,1,0:T(8,128)(2,1)S(1)} %copy-done.18, ...), custom_call_target="tpu_custom_call" | custom-call | flops 754974720 | bytes 2621440 | tf_op jit(solution)/shard_map/score/pallas_call | solution.py:403
  202.4 2.2 %fusion.2 = bf16[128,384]{1,0:T(8,128)(2,1)} fusion(f32[320,128]{1,0:T(8,128)} %get-tuple-element.31, bf16[320,384]{1,0:T(8,128)(2,1)} %bitcast.40, bf16[128,384]{1,0:T(8,128)(2,1)} %param.9), kind=kOutput, calls=%fused_computation.5 | convolution fusion | flops 188891136 | bytes 606208 | tf_op jit(solution)/shard_map/dot_general | solution.py:570
  (163 shorter events, 26.7 us)
Async XLA Ops:
  0.6 40.4 %copy-start.41 = (s32[128]{0:T(128)S(1)}, s32[128]{0:T(128)}, u32[]{:S(2)}) copy-start(s32[128]{0:T(128)} %param.13) | copy-start | bytes 1540
  0.6 30.5 %copy-start.40 = (bf16[384]{0:T(512)(128)(2,1)S(1)}, bf16[384]{0:T(512)(128)(2,1)}, u32[]{:S(2)}) copy-start(bf16[384]{0:T(512)(128)(2,1)} %param.10) | copy-start | bytes 2308
  31.1 23.3 %copy-start.39 = (f32[128,2]{0,1:T(2,128)S(1)}, f32[128,2]{0,1:T(2,128)}, u32[]{:S(2)}) copy-start(f32[128,2]{0,1:T(2,128)} %param.12) | copy-start | bytes 3076
  31.3 9.8 %collective-permute-start.1 = (bf16[656,384]{1,0:T(8,128)(2,1)S(1)}, bf16[656,384]{1,0:T(8,128)(2,1)S(1)}, u32[]{:S(2)}, u32[]{:S(2)}) collective-permute-start(bf16[656,384]{1,0:T(8,128)(2,1)S(1)} %get-tuple-element.46), channel_id=1, source_target_pairs={{0,4},{1,17},{2,6},{3,19},{4,0},{5,21},{6,2},{7,23},{8,12},{9,25},... | collective-permute-start | bytes 1511432 | tf_op jit(solution)/shard_map/ppermute | solution.py:31
  34.3 12.1 %collective-permute-start.2 = (bf16[656,384]{1,0:T(8,128)(2,1)S(1)}, bf16[656,384]{1,0:T(8,128)(2,1)S(1)}, u32[]{:S(2)}, u32[]{:S(2)}) collective-permute-start(bf16[656,384]{1,0:T(8,128)(2,1)S(1)} %get-tuple-element.46), channel_id=1, source_target_pairs={{0,2},{1,9},{2,4},{3,11},{4,6},{5,13},{6,0},{7,15},{8,10},{9,17},{... | collective-permute-start | bytes 1511432 | tf_op jit(solution)/shard_map/ppermute | solution.py:31
  34.7 18.2 %collective-permute-start = (bf16[656,384]{1,0:T(8,128)(2,1)S(1)}, bf16[656,384]{1,0:T(8,128)(2,1)S(1)}, u32[]{:S(2)}, u32[]{:S(2)}) collective-permute-start(bf16[656,384]{1,0:T(8,128)(2,1)S(1)} %get-tuple-element.46), channel_id=1, source_target_pairs={{0,6},{1,25},{2,0},{3,27},{4,2},{5,29},{6,4},{7,31},{8,14},{9,1},{... | collective-permute-start | bytes 1511432 | tf_op jit(solution)/shard_map/ppermute | solution.py:31
  37.0 4.0 %collective-permute-start.9 = (f32[16]{0:T(128)S(1)}, f32[16]{0:T(128)S(1)}, u32[]{:S(2)}, u32[]{:S(2)}) collective-permute-start(f32[16]{0:T(128)S(1)} %fusion.22), channel_id=1, source_target_pairs={{0,1},{1,0},{2,3},{3,2},{4,5},{5,4},{6,7},{7,6},{8,9},{9,8},{10,11... | collective-permute-start | bytes 200 | tf_op jit(solution)/shard_map/ppermute | solution.py:35
  46.5 39.0 %copy-start.19 = (bf16[2,656,384]{2,1,0:T(8,128)(2,1)}, bf16[2,656,384]{2,1,0:T(8,128)(2,1)S(1)}, u32[]{:S(2)}) copy-start(bf16[2,656,384]{2,1,0:T(8,128)(2,1)S(1)} %pad_maximum_fusion.1.refs_1_) | copy-start | bytes 3022852
  46.5 23.2 %collective-permute-start.4 = (bf16[2,656,384]{2,1,0:T(8,128)(2,1)S(1)}, bf16[2,656,384]{2,1,0:T(8,128)(2,1)}, u32[]{:S(2)}, u32[]{:S(2)}) collective-permute-start(bf16[2,656,384]{2,1,0:T(8,128)(2,1)S(1)} %pad_maximum_fusion.1.refs_1_), channel_id=1, source_target_pairs={{0,24},{1,7},{2,26},{3,1},{4,28},{5,3},{6,30},{7,5},{8,0},{9,15},{... | collective-permute-start | bytes 3022856 | tf_op jit(solution)/shard_map/ppermute | solution.py:31
  49.1 25.0 %collective-permute-start.11 = (bf16[2,656,384]{2,1,0:T(8,128)(2,1)S(1)}, bf16[2,656,384]{2,1,0:T(8,128)(2,1)S(1)}, u32[]{:S(2)}, u32[]{:S(2)}) collective-permute-start(bf16[2,656,384]{2,1,0:T(8,128)(2,1)S(1)} %pad_maximum_fusion.1.refs_1_), channel_id=1, source_target_pairs={{0,1},{1,0},{2,3},{3,2},{4,5},{5,4},{6,7},{7,6},{8,9},{9,8},{10,11... | collective-permute-start | bytes 3022856 | tf_op jit(solution)/shard_map/ppermute | solution.py:35
  53.0 20.1 %collective-permute-start.5 = (bf16[2,656,384]{2,1,0:T(8,128)(2,1)S(1)}, bf16[2,656,384]{2,1,0:T(8,128)(2,1)}, u32[]{:S(2)}, u32[]{:S(2)}) collective-permute-start(bf16[2,656,384]{2,1,0:T(8,128)(2,1)S(1)} %pad_maximum_fusion.refs_0_), channel_id=1, source_target_pairs={{0,8},{1,3},{2,10},{3,5},{4,12},{5,7},{6,14},{7,1},{8,16},{9,11},{... | collective-permute-start | bytes 3022856 | tf_op jit(solution)/shard_map/ppermute | solution.py:31
  54.4 22.0 %collective-permute-start.10 = (bf16[2,656,384]{2,1,0:T(8,128)(2,1)S(1)}, bf16[2,656,384]{2,1,0:T(8,128)(2,1)}, u32[]{:S(2)}, u32[]{:S(2)}) collective-permute-start(bf16[2,656,384]{2,1,0:T(8,128)(2,1)S(1)} %pad_maximum_fusion.refs_0_), channel_id=1, source_target_pairs={{0,1},{1,0},{2,3},{3,2},{4,5},{5,4},{6,7},{7,6},{8,9},{9,8},{10,11... | collective-permute-start | bytes 3022856 | tf_op jit(solution)/shard_map/ppermute | solution.py:35
  66.6 2.8 %collective-permute-start.18 = (f32[320,128]{1,0:T(8,128)S(1)}, f32[320,128]{1,0:T(8,128)S(1)}, u32[]{:S(2)}, u32[]{:S(2)}) collective-permute-start(f32[320,128]{1,0:T(8,128)S(1)} %bitcast.178), channel_id=1, source_target_pairs={{0,1},{1,0},{2,3},{3,2},{4,5},{5,4},{6,7},{7,6},{8,9},{9,8},{10,11... | collective-permute-start | bytes 491528 | tf_op jit(solution)/shard_map/ppermute | solution.py:35
  69.5 14.8 %collective-permute-start.8 = (bf16[2,656,384]{2,1,0:T(8,128)(2,1)S(1)}, bf16[2,656,384]{2,1,0:T(8,128)(2,1)}, u32[]{:S(2)}, u32[]{:S(2)}) collective-permute-start(bf16[2,656,384]{2,1,0:T(8,128)(2,1)S(1)} %pad_maximum_fusion.1.refs_1_), channel_id=1, source_target_pairs={{0,8},{1,3},{2,10},{3,5},{4,12},{5,7},{6,14},{7,1},{8,16},{9,11},{... | collective-permute-start | bytes 3022856 | tf_op jit(solution)/shard_map/ppermute | solution.py:31
  69.7 15.8 %collective-permute-start.3 = (bf16[2,656,384]{2,1,0:T(8,128)(2,1)S(1)}, bf16[2,656,384]{2,1,0:T(8,128)(2,1)}, u32[]{:S(2)}, u32[]{:S(2)}) collective-permute-start(bf16[2,656,384]{2,1,0:T(8,128)(2,1)S(1)} %pad_maximum_fusion.refs_0_), channel_id=1, source_target_pairs={{0,24},{1,7},{2,26},{3,1},{4,28},{5,3},{6,30},{7,5},{8,0},{9,15},{... | collective-permute-start | bytes 3022856 | tf_op jit(solution)/shard_map/ppermute | solution.py:31
  73.1 12.5 %collective-permute-start.13 = (bf16[2,656,384]{2,1,0:T(8,128)(2,1)}, bf16[2,656,384]{2,1,0:T(8,128)(2,1)S(1)}, u32[]{:S(2)}, u32[]{:S(2)}) collective-permute-start(bf16[2,656,384]{2,1,0:T(8,128)(2,1)} %collective-permute-done.4.refs_3_.refs_0_), channel_id=1, source_target_pairs={{0,1},{1,0},{2,3},{3,2},{4,5},{5,4},{6,7},{7,6},{8,9},{9,8},{10,11... | collective-permute-start | bytes 3022856 | tf_op jit(solution)/shard_map/ppermute | solution.py:35
  75.0 19.3 %collective-permute-start.7 = (bf16[2,656,384]{2,1,0:T(8,128)(2,1)}, bf16[2,656,384]{2,1,0:T(8,128)(2,1)}, u32[]{:S(2)}, u32[]{:S(2)}) collective-permute-start(bf16[2,656,384]{2,1,0:T(8,128)(2,1)} %collective-permute-done.4.refs_3_.refs_0_), channel_id=1, source_target_pairs={{0,24},{1,7},{2,26},{3,1},{4,28},{5,3},{6,30},{7,5},{8,0},{9,15},{... | collective-permute-start | bytes 3022856 | tf_op jit(solution)/shard_map/ppermute | solution.py:31
  76.4 19.4 %collective-permute-start.6 = (bf16[2,656,384]{2,1,0:T(8,128)(2,1)}, bf16[2,656,384]{2,1,0:T(8,128)(2,1)}, u32[]{:S(2)}, u32[]{:S(2)}) collective-permute-start(bf16[2,656,384]{2,1,0:T(8,128)(2,1)} %collective-permute-done.5.refs_6_.refs_2_.refs_3_), channel_id=1, source_target_pairs={{0,8},{1,3},{2,10},{3,5},{4,12},{5,7},{6,14},{7,1},{8,16},{9,11},{... | collective-permute-start | bytes 3022856 | tf_op jit(solution)/shard_map/ppermute | solution.py:31
  84.3 12.0 %collective-permute-start.16 = (bf16[2,656,384]{2,1,0:T(8,128)(2,1)}, bf16[2,656,384]{2,1,0:T(8,128)(2,1)S(1)}, u32[]{:S(2)}, u32[]{:S(2)}) collective-permute-start(bf16[2,656,384]{2,1,0:T(8,128)(2,1)} %collective-permute-done.5.refs_6_.refs_2_.refs_3_), channel_id=1, source_target_pairs={{0,1},{1,0},{2,3},{3,2},{4,5},{5,4},{6,7},{7,6},{8,9},{9,8},{10,11... | collective-permute-start | bytes 3022856 | tf_op jit(solution)/shard_map/ppermute | solution.py:35
  85.5 11.8 %collective-permute-start.17 = (bf16[2,656,384]{2,1,0:T(8,128)(2,1)}, bf16[2,656,384]{2,1,0:T(8,128)(2,1)S(1)}, u32[]{:S(2)}, u32[]{:S(2)}) collective-permute-start(bf16[2,656,384]{2,1,0:T(8,128)(2,1)} %collective-permute-done.8.refs_7_.refs_1_.refs_0_), channel_id=1, source_target_pairs={{0,1},{1,0},{2,3},{3,2},{4,5},{5,4},{6,7},{7,6},{8,9},{9,8},{10,11... | collective-permute-start | bytes 3022856 | tf_op jit(solution)/shard_map/ppermute | solution.py:35
  86.6 11.7 %collective-permute-start.12 = (bf16[2,656,384]{2,1,0:T(8,128)(2,1)}, bf16[2,656,384]{2,1,0:T(8,128)(2,1)}, u32[]{:S(2)}, u32[]{:S(2)}) collective-permute-start(bf16[2,656,384]{2,1,0:T(8,128)(2,1)} %collective-permute-done.3.refs_2_.refs_0_), channel_id=1, source_target_pairs={{0,1},{1,0},{2,3},{3,2},{4,5},{5,4},{6,7},{7,6},{8,9},{9,8},{10,11... | collective-permute-start | bytes 3022856 | tf_op jit(solution)/shard_map/ppermute | solution.py:35
  94.4 3.9 %collective-permute-start.15 = (bf16[2,656,384]{2,1,0:T(8,128)(2,1)}, bf16[2,656,384]{2,1,0:T(8,128)(2,1)S(1)}, u32[]{:S(2)}, u32[]{:S(2)}) collective-permute-start(bf16[2,656,384]{2,1,0:T(8,128)(2,1)} %collective-permute-done.7.refs_5_.refs_3_.refs_2_), channel_id=1, source_target_pairs={{0,1},{1,0},{2,3},{3,2},{4,5},{5,4},{6,7},{7,6},{8,9},{9,8},{10,11... | collective-permute-start | bytes 3022856 | tf_op jit(solution)/shard_map/ppermute | solution.py:35
  95.9 4.0 %collective-permute-start.14 = (bf16[2,656,384]{2,1,0:T(8,128)(2,1)}, bf16[2,656,384]{2,1,0:T(8,128)(2,1)}, u32[]{:S(2)}, u32[]{:S(2)}) collective-permute-start(bf16[2,656,384]{2,1,0:T(8,128)(2,1)} %collective-permute-done.6.refs_4_.refs_2_.refs_1_), channel_id=1, source_target_pairs={{0,1},{1,0},{2,3},{3,2},{4,5},{5,4},{6,7},{7,6},{8,9},{9,8},{10,11... | collective-permute-start | bytes 3022856 | tf_op jit(solution)/shard_map/ppermute | solution.py:35
  109.7 5.9 %copy-start = (bf16[1,256,6144]{2,1,0:T(8,128)(2,1)S(1)}, bf16[1,256,6144]{2,1,0:T(8,128)(2,1)}, u32[]{:S(2)}) copy-start(bf16[1,256,6144]{2,1,0:T(8,128)(2,1)} %param.17) | copy-start | bytes 9437188
  117.0 3.8 %copy-start.23 = (bf16[2,656,384]{2,1,0:T(8,128)(2,1)S(1)}, bf16[2,656,384]{2,1,0:T(8,128)(2,1)}, u32[]{:S(2)}) copy-start(bf16[2,656,384]{2,1,0:T(8,128)(2,1)} %copy-done.22) | copy-start | bytes 3022852
  119.8 10.6 %collective-permute-start.20 = (bf16[4,320,384]{2,1,0:T(8,128)(2,1)S(1)}, bf16[4,320,384]{2,1,0:T(8,128)(2,1)S(1)}, u32[]{:S(2)}, u32[]{:S(2)}) collective-permute-start(bf16[4,320,384]{2,1,0:T(8,128)(2,1)S(1)} %bitcast.177), channel_id=1, source_target_pairs={{0,1},{1,0},{2,3},{3,2},{4,5},{5,4},{6,7},{7,6},{8,9},{9,8},{10,11... | collective-permute-start | bytes 2949128 | tf_op jit(solution)/shard_map/ppermute | solution.py:35
  120.3 10.1 %collective-permute-start.24 = (bf16[4,320,384]{2,1,0:T(8,128)(2,1)S(1)}, bf16[4,320,384]{2,1,0:T(8,128)(2,1)S(1)}, u32[]{:S(2)}, u32[]{:S(2)}) collective-permute-start(bf16[4,320,384]{2,1,0:T(8,128)(2,1)S(1)} %bitcast.176), channel_id=1, source_target_pairs={{0,1},{1,0},{2,3},{3,2},{4,5},{5,4},{6,7},{7,6},{8,9},{9,8},{10,11... | collective-permute-start | bytes 2949128 | tf_op jit(solution)/shard_map/ppermute | solution.py:35
  120.4 10.0 %collective-permute-start.21 = (bf16[4,320,384]{2,1,0:T(8,128)(2,1)S(1)}, bf16[4,320,384]{2,1,0:T(8,128)(2,1)S(1)}, u32[]{:S(2)}, u32[]{:S(2)}) collective-permute-start(bf16[4,320,384]{2,1,0:T(8,128)(2,1)S(1)} %bitcast.175), channel_id=1, source_target_pairs={{0,1},{1,0},{2,3},{3,2},{4,5},{5,4},{6,7},{7,6},{8,9},{9,8},{10,11... | collective-permute-start | bytes 2949128 | tf_op jit(solution)/shard_map/ppermute | solution.py:35
  131.0 8.1 %collective-permute-start.28 = (bf16[2,320,384]{2,1,0:T(8,128)(2,1)S(1)}, bf16[2,320,384]{2,1,0:T(8,128)(2,1)S(1)}, u32[]{:S(2)}, u32[]{:S(2)}) collective-permute-start(bf16[2,320,384]{2,1,0:T(8,128)(2,1)S(1)} %get-tuple-element.38), channel_id=1, source_target_pairs={{0,24},{1,7},{2,26},{3,1},{4,28},{5,3},{6,30},{7,5},{8,0},{9,15},{... | collective-permute-start | bytes 1474568 | tf_op jit(solution)/shard_map/ppermute | solution.py:31
  133.0 9.2 %collective-permute-start.22 = (bf16[2,320,384]{2,1,0:T(8,128)(2,1)S(1)}, bf16[2,320,384]{2,1,0:T(8,128)(2,1)S(1)}, u32[]{:S(2)}, u32[]{:S(2)}) collective-permute-start(bf16[2,320,384]{2,1,0:T(8,128)(2,1)S(1)} %get-tuple-element.37), channel_id=1, source_target_pairs={{0,8},{1,3},{2,10},{3,5},{4,12},{5,7},{6,14},{7,1},{8,16},{9,11},{... | collective-permute-start | bytes 1474568 | tf_op jit(solution)/shard_map/ppermute | solution.py:31
  134.6 26.9 %collective-permute-start.19 = (bf16[4,320,384]{2,1,0:T(8,128)(2,1)S(1)}, bf16[4,320,384]{2,1,0:T(8,128)(2,1)S(1)}, u32[]{:S(2)}, u32[]{:S(2)}) collective-permute-start(bf16[4,320,384]{2,1,0:T(8,128)(2,1)S(1)} %bitcast.174), channel_id=1, source_target_pairs={{0,1},{1,0},{2,3},{3,2},{4,5},{5,4},{6,7},{7,6},{8,9},{9,8},{10,11... | collective-permute-start | bytes 2949128 | tf_op jit(solution)/shard_map/ppermute | solution.py:35
  136.8 24.6 %collective-permute-start.25 = (bf16[2,320,384]{2,1,0:T(8,128)(2,1)S(1)}, bf16[2,320,384]{2,1,0:T(8,128)(2,1)S(1)}, u32[]{:S(2)}, u32[]{:S(2)}) collective-permute-start(bf16[2,320,384]{2,1,0:T(8,128)(2,1)S(1)} %get-tuple-element.41), channel_id=1, source_target_pairs={{0,24},{1,7},{2,26},{3,1},{4,28},{5,3},{6,30},{7,5},{8,0},{9,15},{... | collective-permute-start | bytes 1474568 | tf_op jit(solution)/shard_map/ppermute | solution.py:31
  138.2 23.3 %collective-permute-start.27 = (bf16[2,320,384]{2,1,0:T(8,128)(2,1)S(1)}, bf16[2,320,384]{2,1,0:T(8,128)(2,1)S(1)}, u32[]{:S(2)}, u32[]{:S(2)}) collective-permute-start(bf16[2,320,384]{2,1,0:T(8,128)(2,1)S(1)} %get-tuple-element.42), channel_id=1, source_target_pairs={{0,8},{1,3},{2,10},{3,5},{4,12},{5,7},{6,14},{7,1},{8,16},{9,11},{... | collective-permute-start | bytes 1474568 | tf_op jit(solution)/shard_map/ppermute | solution.py:31
  142.7 18.8 %collective-permute-start.23 = (bf16[2,320,384]{2,1,0:T(8,128)(2,1)S(1)}, bf16[2,320,384]{2,1,0:T(8,128)(2,1)S(1)}, u32[]{:S(2)}, u32[]{:S(2)}) collective-permute-start(bf16[2,320,384]{2,1,0:T(8,128)(2,1)S(1)} %get-tuple-element.39), channel_id=1, source_target_pairs={{0,8},{1,3},{2,10},{3,5},{4,12},{5,7},{6,14},{7,1},{8,16},{9,11},{... | collective-permute-start | bytes 1474568 | tf_op jit(solution)/shard_map/ppermute | solution.py:31
  143.0 18.5 %collective-permute-start.29 = (bf16[2,320,384]{2,1,0:T(8,128)(2,1)S(1)}, bf16[2,320,384]{2,1,0:T(8,128)(2,1)S(1)}, u32[]{:S(2)}, u32[]{:S(2)}) collective-permute-start(bf16[2,320,384]{2,1,0:T(8,128)(2,1)S(1)} %get-tuple-element.40), channel_id=1, source_target_pairs={{0,24},{1,7},{2,26},{3,1},{4,28},{5,3},{6,30},{7,5},{8,0},{9,15},{... | collective-permute-start | bytes 1474568 | tf_op jit(solution)/shard_map/ppermute | solution.py:31
  148.2 17.9 %copy-start.1 = (bf16[256,6144]{1,0:T(8,128)(2,1)}, bf16[256,6144]{1,0:T(8,128)(2,1)S(1)}, u32[]{:S(2)}) copy-start(bf16[256,6144]{1,0:T(8,128)(2,1)S(1)} %get-tuple-element.28.refs_9_.refs_10_.refs_12_.refs_13_.refs_5_.refs_6_) | copy-start | bytes 9437188
  148.2 17.9 %copy-start.4 = (bf16[256,6144]{1,0:T(8,128)(2,1)}, bf16[256,6144]{1,0:T(8,128)(2,1)S(1)}, u32[]{:S(2)}) copy-start(bf16[256,6144]{1,0:T(8,128)(2,1)S(1)} %get-tuple-element.29.refs_11_.refs_12_.refs_14_.refs_15_.refs_7_.refs_8_) | copy-start | bytes 9437188
  148.4 6.9 %copy-start.13 = (bf16[2,656,384]{2,1,0:T(8,128)(2,1)S(1)}, bf16[2,656,384]{2,1,0:T(8,128)(2,1)}, u32[]{:S(2)}) copy-start(bf16[2,656,384]{2,1,0:T(8,128)(2,1)} %copy-done.11) | copy-start | bytes 3022852
  148.4 6.9 %copy-start.17 = (bf16[2,656,384]{2,1,0:T(8,128)(2,1)S(1)}, bf16[2,656,384]{2,1,0:T(8,128)(2,1)}, u32[]{:S(2)}) copy-start(bf16[2,656,384]{2,1,0:T(8,128)(2,1)} %copy-done.15) | copy-start | bytes 3022852
  161.4 15.2 %copy-start.35 = (bf16[512,640]{1,0:T(8,128)(2,1)}, bf16[512,640]{1,0:T(8,128)(2,1)S(1)}, u32[]{:S(2)}) copy-start(bf16[512,640]{1,0:T(8,128)(2,1)S(1)} %get-tuple-element.26.left_ref) | copy-start | bytes 1966084
  161.9 14.8 %collective-permute-start.26 = (bf16[320,384]{1,0:T(8,128)(2,1)S(1)}, bf16[320,384]{1,0:T(8,128)(2,1)S(1)}, u32[]{:S(2)}, u32[]{:S(2)}) collective-permute-start(bf16[320,384]{1,0:T(8,128)(2,1)S(1)} %get-tuple-element.36), channel_id=1, source_target_pairs={{0,2},{1,9},{2,4},{3,11},{4,6},{5,13},{6,0},{7,15},{8,10},{9,17},{... | collective-permute-start | bytes 737288 | tf_op jit(solution)/shard_map/ppermute | solution.py:31
  162.2 14.5 %collective-permute-start.30 = (bf16[320,384]{1,0:T(8,128)(2,1)S(1)}, bf16[320,384]{1,0:T(8,128)(2,1)S(1)}, u32[]{:S(2)}, u32[]{:S(2)}) collective-permute-start(bf16[320,384]{1,0:T(8,128)(2,1)S(1)} %get-tuple-element.34), channel_id=1, source_target_pairs={{0,4},{1,17},{2,6},{3,19},{4,0},{5,21},{6,2},{7,23},{8,12},{9,25},... | collective-permute-start | bytes 737288 | tf_op jit(solution)/shard_map/ppermute | solution.py:31
  166.0 10.7 %collective-permute-start.31 = (bf16[320,384]{1,0:T(8,128)(2,1)S(1)}, bf16[320,384]{1,0:T(8,128)(2,1)S(1)}, u32[]{:S(2)}, u32[]{:S(2)}) collective-permute-start(bf16[320,384]{1,0:T(8,128)(2,1)S(1)} %get-tuple-element.35), channel_id=1, source_target_pairs={{0,6},{1,25},{2,0},{3,27},{4,2},{5,29},{6,4},{7,31},{8,14},{9,1},{... | collective-permute-start | bytes 737288 | tf_op jit(solution)/shard_map/ppermute | solution.py:31
  177.7 24.7 %all-to-all-start.2 = ((bf16[8,40,384]{2,1,0:T(8,128)(2,1)}), bf16[8,40,384]{2,1,0:T(8,128)(2,1)}, u32[]{:S(2)}, u32[]{:S(2)}) async-start(bf16[8,40,384]{2,1,0:T(8,128)(2,1)} %bitcast.180), calls=%async_computation.2 | async-start | bytes 491520 | tf_op jit(solution)/shard_map/all_to_all | solution.py:499
  190.2 8.0 %copy-start.3 = (bf16[256,6144]{1,0:T(8,128)(2,1)S(1)}, bf16[256,6144]{1,0:T(8,128)(2,1)}, u32[]{:S(2)}) copy-start(bf16[256,6144]{1,0:T(8,128)(2,1)} %copy-done.1) | copy-start | bytes 9437188
  190.2 8.1 %copy-start.6 = (bf16[256,6144]{1,0:T(8,128)(2,1)S(1)}, bf16[256,6144]{1,0:T(8,128)(2,1)}, u32[]{:S(2)}) copy-start(bf16[256,6144]{1,0:T(8,128)(2,1)} %copy-done.4) | copy-start | bytes 9437188
  190.2 8.1 %copy-start.14 = (bf16[2,656,384]{2,1,0:T(8,128)(2,1)S(1)}, bf16[2,656,384]{2,1,0:T(8,128)(2,1)}, u32[]{:S(2)}) copy-start(bf16[2,656,384]{2,1,0:T(8,128)(2,1)} %copy-done.11) | copy-start | bytes 3022852
  190.2 8.1 %copy-start.18 = (bf16[2,656,384]{2,1,0:T(8,128)(2,1)S(1)}, bf16[2,656,384]{2,1,0:T(8,128)(2,1)}, u32[]{:S(2)}) copy-start(bf16[2,656,384]{2,1,0:T(8,128)(2,1)} %copy-done.15) | copy-start | bytes 3022852
  (27 other events, 45.0 us)
